TPU v7x, 128 devices: a whole 4x4x4 slice. The times are simulated.
128 devices in a mesh: grp: 8 (over x, core), dev: 16 (over z, y).
Axes of the slice: x: 4, y: 4, z: 4, core: 2. Of those that a mesh axis runs over, the one named last changes fastest.
Arguments:
- residual: bfloat16 [16384, 2048], P(('grp', 'dev')), may hold values from -3 to 3
- queries: bfloat16 [16384, 1024], P(('grp', 'dev')), may hold values from -9 to 9
- keys: bfloat16 [16384, 256], P(('grp', 'dev')), may hold values from -6 to 6
- values: bfloat16 [16384, 256], P(('grp', 'dev')), may hold values from -18 to 18
- prefix_keys: bfloat16 [32, 1024, 256], P('grp', 'dev'), may hold values from -6 to 6
- cached_prefix_values: bfloat16 [32, 1024, 256], P('grp', 'dev'), may hold values from -18 to 18
- out_weight: bfloat16 [1024, 2048], replicated, may hold values from -0.1875 to 0.1875
- norm_gain: float32 [2048], replicated, may hold values from 0.25 to 1.75
- w_gate: bfloat16 [2048, 8192], P('grp', 'dev'), may hold values from -0.125 to 0.125
- w_up: bfloat16 [2048, 8192], P('grp', 'dev'), may hold values from -0.125 to 0.125
- w_down: bfloat16 [8192, 2048], P('dev', 'grp'), may hold values from -0.0625 to 0.0625
- suffix_lengths: int32 [8, 32], P('grp'), may hold values from 1 to 128, 2048 in all within a row
- request_group: int32 [8, 32], P('grp'), may hold values from 0 to 3, as said below
- placement_order: int32 [8, 32], P('grp'), may hold values from 0 to 31, each once within a row
Outputs:
- layer_out: bfloat16 [16384, 2048], P(('grp', 'dev'))
Inputs may be any that keep to these rules, and one draw needn't show every extreme that they name: `suffix_lengths`: the 32 lengths of one row sum to 2048. `request_group`: each row names each of its 4 groups exactly 8 times. `placement_order`: each row is an ordering of its 32 requests.
All inputs are finite; a program needn't handle non-finite values.
Results may differ from a plain program's by a relative error of at most 0.012.
Values may be sent and summed in bfloat16 or wider, within the bound.
A program may use at most 128 MiB of HBM per device.

v0:
```python
import math

import jax
import jax.numpy as jnp
from jax import lax
from jax.sharding import PartitionSpec as P

HEAD_SIZE = 64


NEG_FILL = -1e30
EPSILON = 1e-05


def row_layout(lengths, group_map, packed_order):
    request_count = lengths.shape[0]
    picked = (packed_order[:, None] == jnp.arange(request_count, dtype=jnp.int32)[None, :]).astype(
        jnp.int32
    )
    packed_len = jnp.sum(picked * lengths[None, :], axis=1)
    packed_group = jnp.sum(picked * group_map[None, :], axis=1)
    ends_at = jnp.cumsum(packed_len)
    return (ends_at - packed_len, ends_at, packed_group)


def token_info(token_rows, starts_at, ends_at, packed_group):
    inside = (
        (token_rows[:, None] >= starts_at[None, :]) & (token_rows[:, None] < ends_at[None, :])
    ).astype(jnp.int32)
    return (
        jnp.sum(inside * packed_group[None, :], axis=1),
        jnp.sum(inside * starts_at[None, :], axis=1),
    )


def block_partial(rows_of_queries, allowed, rows_of_keys, rows_of_values):
    query_row_count = rows_of_queries.shape[0]
    key_row_count = rows_of_keys.shape[0]
    heads_kv = rows_of_keys.shape[1] // HEAD_SIZE
    heads_of_queries = rows_of_queries.reshape(query_row_count, heads_kv, -1, HEAD_SIZE)
    heads_of_keys = rows_of_keys.reshape(key_row_count, heads_kv, HEAD_SIZE)
    heads_of_values = rows_of_values.reshape(key_row_count, heads_kv, HEAD_SIZE)
    scores = jnp.einsum(
        "nkrd,mkd->nkrm", heads_of_queries, heads_of_keys, preferred_element_type=jnp.float32
    ) * HEAD_SIZE ** (-0.5)
    scores = jnp.where(allowed[:, None, None, :], scores, NEG_FILL)
    maxima = jnp.max(scores, axis=-1)
    weights = jnp.exp(scores - maxima[..., None])
    totals = jnp.sum(weights, axis=-1)
    numerator = jnp.einsum(
        "nkrm,mkd->nkrd",
        weights.astype(jnp.bfloat16),
        heads_of_values,
        preferred_element_type=jnp.float32,
    )
    return (numerator / totals[..., None], maxima, totals)


def merge_all(local_output, local_maximum, local_sum, block_outs, block_maxima, block_sums):
    highest = jnp.maximum(local_maximum, jnp.max(block_maxima, axis=0))
    own_scale = local_sum * jnp.exp(local_maximum - highest)
    scales = block_sums * jnp.exp(block_maxima - highest[None])
    numerator = own_scale[..., None] * local_output + jnp.sum(
        scales[..., None] * block_outs.astype(jnp.float32), axis=0
    )
    return numerator / (own_scale + jnp.sum(scales, axis=0))[..., None]


def shards(
    residual,
    queries,
    keys,
    values,
    prefix_keys,
    cached_prefix_values,
    out_weight,
    norm_gain,
    w_gate,
    w_up,
    w_down,
    suffix_lengths,
    request_group,
    placement_order,
):
    tok_rows = queries.shape[0]
    key_value_width = keys.shape[1]
    span = prefix_keys.shape[1]
    block_keys = prefix_keys.shape[0] * span
    starts_at, ends_at, packed_group = row_layout(
        suffix_lengths[0], request_group[0], placement_order[0]
    )
    base_row = lax.axis_index("dev") * tok_rows
    own_rows = base_row + jnp.arange(tok_rows, dtype=jnp.int32)
    own_group, own_start = token_info(own_rows, starts_at, ends_at, packed_group)
    window = base_row - tok_rows + jnp.arange(2 * tok_rows, dtype=jnp.int32)
    suffix_mask = (window[None, :] >= own_start[:, None]) & (window[None, :] <= own_rows[:, None])
    key_group = jnp.arange(block_keys, dtype=jnp.int32) // span
    row_queries, row_keys, row_values = (
        lax.all_gather(queries, "dev", axis=0, tiled=True),
        lax.all_gather(keys, "dev", axis=0, tiled=True),
        lax.all_gather(values, "dev", axis=0, tiled=True),
    )
    prior_row = jnp.maximum(base_row - tok_rows, 0)
    before_keys = lax.dynamic_slice_in_dim(row_keys, prior_row, tok_rows, 0)
    before_values = lax.dynamic_slice_in_dim(row_values, prior_row, tok_rows, 0)
    local_output, local_maximum, local_sum = block_partial(
        queries,
        suffix_mask,
        jnp.concatenate([before_keys, keys], axis=0),
        jnp.concatenate([before_values, values], axis=0),
    )
    flat_keys = prefix_keys.reshape(block_keys, key_value_width)
    flat_values = cached_prefix_values.reshape(block_keys, key_value_width)
    row_count = row_queries.shape[0]
    row_group = token_info(
        jnp.arange(row_count, dtype=jnp.int32), starts_at, ends_at, packed_group
    )[0]
    step_rows = math.gcd(row_count, 512)

    def owner_block(block_index):
        first_row = block_index * step_rows
        rows_of_queries = lax.dynamic_slice_in_dim(row_queries, first_row, step_rows, 0)
        group_rows = lax.dynamic_slice_in_dim(row_group, first_row, step_rows, 0)
        allowed = group_rows[:, None] == key_group[None, :]
        part_out, maxima, totals = block_partial(rows_of_queries, allowed, flat_keys, flat_values)
        return (
            part_out.astype(jnp.bfloat16).reshape(step_rows, -1),
            maxima.reshape(step_rows, -1),
            totals.reshape(step_rows, -1),
        )

    part_outs, part_maxima, part_sums = lax.map(
        owner_block, jnp.arange(row_count // step_rows, dtype=jnp.int32)
    )
    peers = row_count // tok_rows
    part_outs = part_outs.reshape(peers, tok_rows, -1)
    part_maxima = part_maxima.reshape(peers, tok_rows, -1)
    part_sums = part_sums.reshape(peers, tok_rows, -1)
    back_outs = lax.all_to_all(part_outs, "dev", split_axis=0, concat_axis=0, tiled=True)
    back_maxima, back_sums = (
        lax.all_to_all(part_maxima, "dev", split_axis=0, concat_axis=0, tiled=True),
        lax.all_to_all(part_sums, "dev", split_axis=0, concat_axis=0, tiled=True),
    )
    merged = merge_all(
        local_output,
        local_maximum,
        local_sum,
        back_outs.reshape((peers,) + local_output.shape),
        back_maxima.reshape((peers,) + local_maximum.shape),
        back_sums.reshape((peers,) + local_sum.shape),
    )
    attention = merged.astype(jnp.bfloat16).reshape(tok_rows, -1)
    hidden_state = residual.astype(jnp.float32) + jnp.dot(
        attention, out_weight, preferred_element_type=jnp.float32
    )
    normed = (
        hidden_state
        * lax.rsqrt(jnp.mean(hidden_state * hidden_state, axis=-1, keepdims=True) + EPSILON)
        * norm_gain
    ).astype(jnp.bfloat16)
    full_gate, full_up, full_down = (
        lax.all_gather(w_gate, "grp", axis=0, tiled=True),
        lax.all_gather(w_up, "grp", axis=0, tiled=True),
        lax.all_gather(w_down, "grp", axis=1, tiled=True),
    )
    shard_piece = lax.all_gather(normed, "dev", axis=0, tiled=True)
    gate_value = jnp.dot(shard_piece, full_gate, preferred_element_type=jnp.float32)
    up_value = jnp.dot(shard_piece, full_up, preferred_element_type=jnp.float32)
    activation = (jax.nn.silu(gate_value) * up_value).astype(jnp.bfloat16)
    mlp_sum = lax.psum_scatter(
        jnp.dot(activation, full_down, preferred_element_type=jnp.float32).astype(jnp.bfloat16),
        "dev",
        scatter_dimension=0,
        tiled=True,
    ).astype(jnp.float32)
    return (hidden_state + mlp_sum).astype(jnp.bfloat16)


def solution(mesh):
    placed = (
        P(("grp", "dev"), None),
        P(("grp", "dev"), None),
        P(("grp", "dev"), None),
        P(("grp", "dev"), None),
        P("grp", "dev", None),
        P("grp", "dev", None),
        P(),
        P(),
        P("grp", "dev"),
        P("grp", "dev"),
        P("dev", "grp"),
        P("grp", None),
        P("grp", None),
        P("grp", None),
    )
    return jax.shard_map(
        shards, mesh=mesh, in_specs=placed, out_specs=P(("grp", "dev"), None), check_vma=False
    )
```

profile of v0, /device:TPU:0, one launch (start us, length us, event | category | flops | bytes accessed | tf_op | source)
XLA Modules:
  0.0 460.7 jit_solution(9504915503423663527)
XLA Ops:
  6.5 1.8 copy.63
  11.2 57.8 %all-gather.10.cloned.1.call-done = bf16[2048,1024]{0,1:T(8,128)(2,1)} async-done(((bf16[128,1024]{0,1:T(8,128)(2,1)}), bf16[2048,1024]{0,1:T(8,128)(2,1)}) %all-gather.10.cloned.1.call-update) | async-done | bytes 4194320 | tf_op jit(solution)/shard_map/all_gather | solution.py:99
  69.0 64.9 %while.15 = (s32[]{:T(128)}, bf16[4,512,1024]{2,1,0:T(8,128)(2,1)}, f32[4,512,16]{1,0,2:T(4,128)S(1)}, f32[4,512,16]{1,0,2:T(4,128)S(1)}, s32[4]{0:T(128)S(1)}, ...) while((s32[]{:T(128)}, bf16[4,512,1024]{2,1,0:T(8,128)(2,1)}, ...), condition=%wide.region_10.11_spmd.clone, body=%wide.region_7.10_spmd.clone.sunk | while | flops 561104896 | bytes 69378800 | solution.py:132
  74.1 1.8 fusion.50
  75.9 1.4 copy-done
  77.5 5.6 %fusion.51 = bf16[512,4,4,64]{0,3,2,1:T(8,128)(2,1)S(1)} fusion(f32[4,512,4,256]{1,3,2,0:T(8,128)} %copy-done, f32[512,4,4]{0,2,1:T(4,128)S(1)} %get-tuple-element.183, pred[512,256]{0,1:T(8,128)(4,1)S(1)} %broadcast_compare_fusion.2, f32[512,4,4]{0,2,1:T(4,128)S(1)} %fusion.50, bf16[256,4,64,1]{2,1,0,3:T(4,128)(2,1)S(1)} %bitcast.111), kind=kOutput, calls=%fused_computation.10.clone.1 | convolution fusion | flops 277872640 | bytes 9764864 | tf_op jit(solution)/shard_map/while/body/eval_jaxpr/nkrm,mkd->nkrd/dot_general | solution.py:50
  89.0 1.4 bitcast_reduce_fusion.2
  90.4 1.8 fusion.50
  92.2 1.4 copy-done
  93.8 5.6 %fusion.51 = bf16[512,4,4,64]{0,3,2,1:T(8,128)(2,1)S(1)} fusion(f32[4,512,4,256]{1,3,2,0:T(8,128)} %copy-done, f32[512,4,4]{0,2,1:T(4,128)S(1)} %get-tuple-element.183, pred[512,256]{0,1:T(8,128)(4,1)S(1)} %broadcast_compare_fusion.2, f32[512,4,4]{0,2,1:T(4,128)S(1)} %fusion.50, bf16[256,4,64,1]{2,1,0,3:T(4,128)(2,1)S(1)} %bitcast.111), kind=kOutput, calls=%fused_computation.10.clone.1 | convolution fusion | flops 277872640 | bytes 9764864 | tf_op jit(solution)/shard_map/while/body/eval_jaxpr/nkrm,mkd->nkrd/dot_general | solution.py:50
  105.2 1.4 bitcast_reduce_fusion.2
  106.6 1.8 fusion.50
  108.4 1.4 copy-done
  110.0 5.6 %fusion.51 = bf16[512,4,4,64]{0,3,2,1:T(8,128)(2,1)S(1)} fusion(f32[4,512,4,256]{1,3,2,0:T(8,128)} %copy-done, f32[512,4,4]{0,2,1:T(4,128)S(1)} %get-tuple-element.183, pred[512,256]{0,1:T(8,128)(4,1)S(1)} %broadcast_compare_fusion.2, f32[512,4,4]{0,2,1:T(4,128)S(1)} %fusion.50, bf16[256,4,64,1]{2,1,0,3:T(4,128)(2,1)S(1)} %bitcast.111), kind=kOutput, calls=%fused_computation.10.clone.1 | convolution fusion | flops 277872640 | bytes 9764864 | tf_op jit(solution)/shard_map/while/body/eval_jaxpr/nkrm,mkd->nkrd/dot_general | solution.py:50
  122.9 1.8 fusion.50
  124.6 1.4 copy-done
  126.2 5.6 %fusion.51 = bf16[512,4,4,64]{0,3,2,1:T(8,128)(2,1)S(1)} fusion(f32[4,512,4,256]{1,3,2,0:T(8,128)} %copy-done, f32[512,4,4]{0,2,1:T(4,128)S(1)} %get-tuple-element.183, pred[512,256]{0,1:T(8,128)(4,1)S(1)} %broadcast_compare_fusion.2, f32[512,4,4]{0,2,1:T(4,128)S(1)} %fusion.50, bf16[256,4,64,1]{2,1,0,3:T(4,128)(2,1)S(1)} %bitcast.111), kind=kOutput, calls=%fused_computation.10.clone.1 | convolution fusion | flops 277872640 | bytes 9764864 | tf_op jit(solution)/shard_map/while/body/eval_jaxpr/nkrm,mkd->nkrd/dot_general | solution.py:50
  134.6 4.9 %all-to-all-start = ((f32[16,128,16]{1,2,0:T(8,128)}), f32[16,128,16]{1,2,0:T(8,128)S(1)}, u32[]{:S(2)}, u32[]{:S(2)}) async-start(f32[16,128,16]{1,2,0:T(8,128)} %copy.66), calls=%async_computation | async-start | bytes 262144 | tf_op jit(solution)/shard_map/all_to_all | solution.py:141
  140.3 7.2 %all-to-all-done = f32[16,128,16]{1,2,0:T(8,128)S(1)} async-done(((f32[16,128,16]{1,2,0:T(8,128)}), f32[16,128,16]{1,2,0:T(8,128)S(1)}, u32[]{:S(2)}, u32[]{:S(2)}) %all-to-all-start) | async-done | bytes 131104 | tf_op jit(solution)/shard_map/all_to_all | solution.py:141
  147.6 3.5 all-to-all-start.1
  151.1 6.4 %copy.75 = bf16[16,128,1024]{1,2,0:T(8,128)(2,1)} copy(bf16[16,128,1024]{2,1,0:T(8,128)(2,1)} %bitcast.112) | data formatting | bytes 8388608 | tf_op jit(solution)/shard_map/reshape | solution.py:136
  157.5 1.9 all-to-all-done.1
  159.4 5.4 %all-to-all-start.2 = ((bf16[16,128,1024]{1,2,0:T(8,128)(2,1)}), bf16[16,128,1024]{1,2,0:T(8,128)(2,1)}, u32[]{:S(2)}, u32[]{:S(2)}) async-start(bf16[16,128,1024]{1,2,0:T(8,128)(2,1)} %copy.75), calls=%async_computation.2 | async-start | bytes 8388608 | tf_op jit(solution)/shard_map/all_to_all | solution.py:139
  168.3 50.7 %all-to-all-done.2 = bf16[16,128,1024]{1,2,0:T(8,128)(2,1)} async-done(((bf16[16,128,1024]{1,2,0:T(8,128)(2,1)}), bf16[16,128,1024]{1,2,0:T(8,128)(2,1)}, u32[]{:S(2)}, u32[]{:S(2)}) %all-to-all-start.2) | async-done | bytes 4194336 | tf_op jit(solution)/shard_map/all_to_all | solution.py:139
  219.0 3.2 fusion.16
  226.0 68.2 %all-gather.14.cloned.1.call-done = bf16[2048,2048]{1,0:T(8,128)(2,1)} async-done(((bf16[128,2048]{1,0:T(8,128)(2,1)}), bf16[2048,2048]{1,0:T(8,128)(2,1)}) %all-gather.14.cloned.1.call-update) | async-done | bytes 8388624 | tf_op jit(solution)/shard_map/all_gather | solution.py:166
  294.2 10.4 %fusion.30 = f32[2048,512]{1,0:T(8,128)} fusion(bf16[2048,2048]{1,0:T(8,128)(2,1)} %all-gather.14.cloned.1.call-done, bf16[2048,512]{1,0:T(8,128)(2,1)} %all-gather.16.cloned.1.call-done), kind=kOutput, calls=%fused_computation.64 | convolution fusion | flops 4294967296 | bytes 14680064 | tf_op jit(solution)/shard_map/dot_general | solution.py:167
  304.6 16.0 %all-gather.18.cloned.1.call-done = bf16[2048,512]{1,0:T(8,128)(2,1)} async-done(((bf16[256,512]{1,0:T(8,128)(2,1)}), bf16[2048,512]{1,0:T(8,128)(2,1)}) %all-gather.18.cloned.1.call-update) | async-done | bytes 2097168 | tf_op jit(solution)/shard_map/all_gather | solution.py:163
  320.6 28.9 %all-gather.20.cloned.1.call-done = bf16[512,2048]{1,0:T(8,128)(2,1)} async-done(((bf16[512,256]{1,0:T(8,128)(2,1)}), bf16[512,2048]{1,0:T(8,128)(2,1)}) %all-gather.20.cloned.1.call-update) | async-done | bytes 2097168 | tf_op jit(solution)/shard_map/all_gather | solution.py:164
  349.5 15.2 %convolution_convert_fusion = bf16[2048,2048]{1,0:T(8,128)(2,1)} fusion(bf16[512,2048]{1,0:T(8,128)(2,1)} %all-gather.20.cloned.1.call-done, f32[2048,512]{1,0:T(8,128)} %fusion.30, bf16[2048,2048]{1,0:T(8,128)(2,1)} %all-gather.14.cloned.1.call-done, bf16[2048,512]{1,0:T(8,128)(2,1)} %all-gather.18.cloned.1.call-done), kind=kOutput, calls=%fused_computation.25 | convolution fusion | flops 8600420352 | bytes 25165824 | tf_op jit(solution)/shard_map/dot_general | solution.py:171
  364.8 87.2 %reduce-scatter.2.cloned.1.call-done = bf16[128,2048]{1,0:T(8,128)(2,1)} async-done(((bf16[2048,2048]{1,0:T(8,128)(2,1)}), bf16[128,2048]{1,0:T(8,128)(2,1)}) %reduce-scatter.2.cloned.1.call-update) | async-done | bytes 524304 | tf_op jit(solution)/shard_map/reduce_scatter | solution.py:170
  451.9 1.9 add_convert_fusion
  (134 shorter events, 35.6 us)
Async XLA Ops:
  6.5 62.4 %all-gather.10.cloned.1.call-start = ((), (), s32[]{:S(2)}) async-start(), calls=%async_computation.5 | async-start | bytes 4456448 | tf_op jit(solution)/shard_map/all_gather | solution.py:99
  8.4 157.6 %all-gather.12.cloned.1.call-start = ((), (), s32[]{:S(2)}) async-start(), calls=%async_computation.6 | async-start | bytes 1114112 | tf_op jit(solution)/shard_map/all_gather | solution.py:101
  9.1 156.8 %all-gather.8.cloned.1.call-start = ((), (), s32[]{:S(2)}) async-start(), calls=%async_computation.4 | async-start | bytes 1114112 | tf_op jit(solution)/shard_map/all_gather | solution.py:100
  74.1 3.2 copy-start
  74.1 3.2 copy-start.2
  90.4 3.2 copy-start
  90.4 3.2 copy-start.2
  106.6 3.2 copy-start
  106.6 3.2 copy-start.2
  122.8 3.2 copy-start
  122.9 3.2 copy-start.2
  134.6 12.9 %all-to-all-start = ((f32[16,128,16]{1,2,0:T(8,128)}), f32[16,128,16]{1,2,0:T(8,128)S(1)}, u32[]{:S(2)}, u32[]{:S(2)}) async-start(f32[16,128,16]{1,2,0:T(8,128)} %copy.66), calls=%async_computation | async-start | bytes 262144 | tf_op jit(solution)/shard_map/all_to_all | solution.py:141
  147.6 11.8 %all-to-all-start.1 = ((f32[16,128,16]{1,2,0:T(8,128)}), f32[16,128,16]{1,2,0:T(8,128)S(1)}, u32[]{:S(2)}, u32[]{:S(2)}) async-start(f32[16,128,16]{1,2,0:T(8,128)} %copy.70), calls=%async_computation.1 | async-start | bytes 262144 | tf_op jit(solution)/shard_map/all_to_all | solution.py:142
  157.5 9.4 %copy-start.5 = (bf16[128,256]{1,0:T(8,128)(2,1)S(1)}, bf16[128,256]{1,0:T(8,128)(2,1)}, u32[]{:S(2)}) copy-start(bf16[128,256]{1,0:T(8,128)(2,1)} %param.18) | copy-start | bytes 196612
  157.5 9.5 %copy-start.6 = (bf16[128,256]{1,0:T(8,128)(2,1)S(1)}, bf16[128,256]{1,0:T(8,128)(2,1)}, u32[]{:S(2)}) copy-start(bf16[128,256]{1,0:T(8,128)(2,1)} %param.19) | copy-start | bytes 196612
  157.5 9.7 %copy-start.3 = (bf16[128,1024]{0,1:T(8,128)(2,1)S(1)}, bf16[128,1024]{0,1:T(8,128)(2,1)}, u32[]{:S(2)}) copy-start(bf16[128,1024]{0,1:T(8,128)(2,1)} %copy.63) | copy-start | bytes 786436
  159.4 59.6 %all-to-all-start.2 = ((bf16[16,128,1024]{1,2,0:T(8,128)(2,1)}), bf16[16,128,1024]{1,2,0:T(8,128)(2,1)}, u32[]{:S(2)}, u32[]{:S(2)}) async-start(bf16[16,128,1024]{1,2,0:T(8,128)(2,1)} %copy.75), calls=%async_computation.2 | async-start | bytes 8388608 | tf_op jit(solution)/shard_map/all_to_all | solution.py:139
  164.9 61.1 %all-gather.16.cloned.1.call-start = ((), (), s32[]{:S(2)}) async-start(), calls=%async_computation.8 | async-start | bytes 2359296 | tf_op jit(solution)/shard_map/all_gather | solution.py:162
  165.4 128.8 %all-gather.14.cloned.1.call-start = ((), (), s32[]{:S(2)}) async-start(), calls=%async_computation.7 | async-start | bytes 8912896 | tf_op jit(solution)/shard_map/all_gather | solution.py:166
  168.3 54.4 %copy-start.4 = (bf16[128,2048]{1,0:T(8,128)(2,1)S(1)}, bf16[128,2048]{1,0:T(8,128)(2,1)}, u32[]{:S(2)}) copy-start(bf16[128,2048]{1,0:T(8,128)(2,1)} %param.16) | copy-start | bytes 1572868
  219.0 3.7 copy-start.1
  222.7 0.9 copy-start.7
  224.6 96.1 %all-gather.18.cloned.1.call-start = ((), (), s32[]{:S(2)}) async-start(), calls=%async_computation.9 | async-start | bytes 2359296 | tf_op jit(solution)/shard_map/all_gather | solution.py:163
  225.2 124.3 %all-gather.20.cloned.1.call-start = ((), (), s32[]{:S(2)}) async-start(), calls=%async_computation.10 | async-start | bytes 2359296 | tf_op jit(solution)/shard_map/all_gather | solution.py:164
  225.9 226.0 %reduce-scatter.2.cloned.1.call-start = ((), (), s32[]{:S(2)}) async-start(), calls=%async_computation.11 | async-start | bytes 8912896 | tf_op jit(solution)/shard_map/reduce_scatter | solution.py:170
Sparse Core Ops, SparseCore 0:
  9.4 59.4 all-gather.9
  71.1 41.8 all-gather.11
  115.2 42.2 all-gather.7
  167.1 26.6 all-gather.15
  224.7 69.4 all-gather.13
  295.8 24.8 all-gather.17
  322.3 27.1 all-gather.19
  364.9 87.0 reduce-scatter.1
where the time goes:
time: 462 us; the launch traced here: 461 us
  waiting for transfers between devices  321 us (69%)
  matrix products  55.4 us (12%)
  local copies, waits for them, and re-layouts  37.8 us (8%)
  other arithmetic  15.6 us (3%)
  starting transfers between devices  14.3 us (3%)
  between operations  13.8 us (3%)
    reduce_scatter x1, waiting for transfers between devices, shards(): lax.psum_scatter(jnp.dot(activation, full_down, preferred_element_type=jn...  87.2 us
    all_gather x1, waiting for transfers between devices, shards(): shard_piece = lax.all_gather(normed, 'dev', axis=0, tiled=True)  68.2 us
    all_gather x1, waiting for transfers between devices, shards(): lax.all_gather(queries, 'dev', axis=0, tiled=True)  57.8 us
    all_to_all x1, waiting for transfers between devices, shards(): lax.all_to_all(part_outs, 'dev', split_axis=0, concat_axis=0, tiled=True)  50.7 us
    all_gather x1, waiting for transfers between devices, shards(): lax.all_gather(w_down, 'grp', axis=1, tiled=True)  28.9 us
    dot_general x5, matrix products, block_partial(): jnp.einsum('nkrm,mkd->nkrd', weights.astype(jnp.bfloat16), heads_of_value...  22.8 us
    all_gather x1, waiting for transfers between devices, shards(): lax.all_gather(w_up, 'grp', axis=0, tiled=True)  16 us
    dot_general x1, matrix products, shards(): jnp.dot(activation, full_down, preferred_element_type=jnp.float32)  15.2 us
  transfers between devices with their start and end apart: 11, of which 8 were waited for; matrix products, arithmetic and copies ran while one was open for 18% of the time, Pallas kernels for 0%

commit v1 on v0

v1 whole, which is shorter than its diff:
```python
import jax
import jax.numpy as jnp
from jax import lax
from jax.experimental import pallas as pl
from jax.experimental.pallas import tpu as pltpu
from jax.sharding import PartitionSpec as P

EPSILON = 1e-05
NEG_FILL = -1e30
MESH = pl.DeviceIdType.MESH
F32, BF16 = jnp.float32, jnp.bfloat16
N_SEM = 104


def token_info(lengths, groups, order, first_row):
    n = lengths.shape[1]
    rows = lax.broadcasted_iota(jnp.int32, (n, n), 0)
    cols = lax.broadcasted_iota(jnp.int32, (n, n), 1)
    diagonal = rows == cols

    def column(row):
        spread = jnp.broadcast_to(row, (n, n))
        return jnp.sum(jnp.where(diagonal, spread, 0.0), axis=1, keepdims=True)

    picked = jnp.broadcast_to(order, (n, n)) == rows
    packed_len = jnp.sum(jnp.where(picked, column(lengths), 0.0), axis=0, keepdims=True)
    packed_group = jnp.sum(jnp.where(picked, column(groups), 0.0), axis=0, keepdims=True)
    ends = jnp.sum(jnp.where(rows <= cols, column(packed_len), 0.0), axis=0, keepdims=True)
    starts = ends - packed_len
    token = (lax.broadcasted_iota(jnp.int32, (128, n), 0) + first_row).astype(F32)
    inside = (token >= starts) & (token < ends)
    group = jnp.sum(jnp.where(inside, packed_group, 0.0), axis=1, keepdims=True)
    start = jnp.sum(jnp.where(inside, starts, 0.0), axis=1, keepdims=True)
    return group, start


def kernel(
    res_in, q_in, k_in, v_in, pk_in, pv_in, ow_in, gain_in, wg_in, wu_in, wd_in, len_in, grp_in, ord_in,
    out,
    kbuf, vbuf, kprev, vprev, ks, vs, attn, owb, resb, hid, xn, wg, wu, wd, act, acc, stage, back,
    ssem, rsem, lsem,
):
    gi, di = lax.axis_index("grp"), lax.axis_index("dev")
    x, c = gi // 2, lax.rem(gi, 2)
    z, y = di // 4, lax.rem(di, 4)

    def at(xx, cc, zz, yy):
        return (lax.rem(xx + 4, 4) * 2 + cc, lax.rem(zz + 4, 4) * 4 + lax.rem(yy + 4, 4))

    xs = {k: at(x + k, c, z, y) for k in (1, -1)}
    ys = {k: at(x, c, z, y + k) for k in (1, -1)}
    zs = {k: at(x, c, z + k, y) for k in (1, -1, 2)}
    partner = (x * 2 + (1 - c), di)
    following, preceding = (gi, lax.rem(di + 1, 16)), (gi, lax.rem(di + 15, 16))
    peers = [xs[1], xs[-1], ys[1], ys[-1], zs[1], zs[-1], zs[2], partner, following, preceding]

    barrier = pltpu.get_barrier_semaphore()
    for peer in peers:
        pl.semaphore_signal(barrier, inc=1, device_id=peer, device_id_type=MESH)
    pl.semaphore_wait(barrier, len(peers))

    started = []
    counter = [0]

    def send(src, dst, device):
        i = counter[0]
        counter[0] += 1
        copy = pltpu.make_async_remote_copy(
            src_ref=src, dst_ref=dst, send_sem=ssem.at[i], recv_sem=rsem.at[i],
            device_id=device, device_id_type=MESH,
        )
        copy.start()
        started.append(copy)
        return copy

    local_count = [0]

    def bring(src, dst):
        i = local_count[0]
        local_count[0] += 1
        copy = pltpu.make_async_copy(src, dst, lsem.at[i])
        copy.start()
        return copy

    class Ring:
        def __init__(self, where, pos, slot, half):
            self.where, self.pos, self.slot, self.half = where, pos, slot, half

        def start(self, src=None):
            mine = self.slot(self.pos)
            src = mine if src is None else src
            self.up = send(src, mine, self.where[1])
            self.down = send(src, mine, self.where[-1])

        def relay(self):
            before, after = lax.rem(self.pos + 3, 4), lax.rem(self.pos + 1, 4)
            self.up.wait_recv()
            self.a = send(self.half(before, 0), self.half(before, 0), self.where[1])
            self.down.wait_recv()
            self.b = send(self.half(after, 1), self.half(after, 1), self.where[-1])

        def finish(self):
            self.a.wait_recv()
            self.b.wait_recv()

        def around(self):
            return [lax.rem(self.pos + k, 4) for k in (3, 1, 2)]

    gate1 = Ring(xs, x, lambda i: wg.at[y, i, c], lambda i, h: wg.at[y, i, c, pl.ds(128 * h, 128)])
    gate2 = Ring(ys, y, lambda i: wg.at[i, :, c], lambda i, h: wg.at[i, pl.ds(2 * h, 2), c])
    up1 = Ring(ys, y, lambda i: wu.at[i, x, c], lambda i, h: wu.at[i, x, c, pl.ds(128 * h, 128)])
    up2 = Ring(xs, x, lambda i: wu.at[:, i, c], lambda i, h: wu.at[pl.ds(2 * h, 2), i, c])
    down1 = Ring(ys, y, lambda i: wd.at[x, c, i], lambda i, h: wd.at[x, c, i, pl.ds(256 * h, 256)])
    down2 = Ring(xs, x, lambda i: wd.at[i, c], lambda i, h: wd.at[i, c, pl.ds(2 * h, 2)])
    key1 = Ring(ys, y, lambda i: kbuf.at[z, i], lambda i, h: kbuf.at[z, i, pl.ds(2 * h, 2)])
    key2 = Ring(zs, z, lambda i: kbuf.at[i], lambda i, h: kbuf.at[i, pl.ds(2 * h, 2)])
    val1 = Ring(zs, z, lambda i: vbuf.at[i, y], lambda i, h: vbuf.at[i, y, pl.ds(2 * h, 2)])
    val2 = Ring(ys, y, lambda i: vbuf.at[:, i], lambda i, h: vbuf.at[pl.ds(2 * h, 2), i])

    gate1.start(wg_in)
    local_gate = bring(wg_in, wg.at[y, x, c])
    local_up = bring(wu_in, wu.at[y, x, c])
    local_down = bring(wd_in, wd.at[x, c, y])
    local_out = bring(ow_in, owb)
    local_res = bring(res_in, resb)
    next_k = send(k_in, kprev, following)
    next_v = send(v_in, vprev, following)

    low64 = lax.broadcasted_iota(jnp.int32, (64, 128), 1) < 64
    for src, dst in ((pk_in, kbuf), (pv_in, vbuf)):
        for h in range(4):
            cut = slice(128 * (h // 2), 128 * (h // 2) + 128)
            pairs = []
            for g in (0, 2):
                a, b = src[g, :, cut].astype(F32), src[g + 1, :, cut].astype(F32)
                if h % 2 == 0:
                    pairs.append(jnp.where(low64, a, pltpu.roll(b, 64, 1)))
                else:
                    pairs.append(jnp.where(low64, pltpu.roll(a, 64, 1), b))
            dst[z, y, h] = jnp.concatenate(pairs, axis=1).astype(BF16)
    key1.start()
    val1.start()
    up1.start(wu_in)

    first_row = di * 128
    group, start = token_info(
        len_in[...].astype(F32), grp_in[...].astype(F32), ord_in[...], first_row
    )
    lane_group = (lax.broadcasted_iota(jnp.int32, (128, 256), 1) // 64).astype(F32)
    in_group = (lane_group == group).astype(F32)
    window = (lax.broadcasted_iota(jnp.int32, (128, 256), 1) + (first_row - 128)).astype(F32)
    token = (lax.broadcasted_iota(jnp.int32, (128, 256), 0) + first_row).astype(F32)
    bias = jnp.where((window >= start) & (window <= token), 0.0, NEG_FILL)
    low = lax.broadcasted_iota(jnp.int32, (128, 128), 1) < 64

    def twice(block):
        turned = pltpu.roll(block, 64, 1)
        first, second = jnp.where(low, block, turned), jnp.where(low, turned, block)
        return jnp.concatenate([first, first], axis=1), jnp.concatenate([second, second], axis=1)

    def spread(src, dst, row):
        for b in (0, 1):
            first, second = twice(src[:, 128 * b:128 * b + 128].astype(F32))
            dst[2 * b, row:row + 128] = first.astype(BF16)
            dst[2 * b + 1, row:row + 128] = second.astype(BF16)

    spread(k_in, ks, 128)
    spread(v_in, vs, 128)

    key1.relay()
    val1.relay()
    up1.relay()
    val1.finish()
    val2.start()
    key1.finish()
    key2.start()
    down1.start(wd_in)
    gate1.relay()

    next_k.wait_recv()
    next_v.wait_recv()
    spread(kprev, ks, 0)
    spread(vprev, vs, 0)

    up1.finish()
    local_up.wait()
    up2.start()
    up_share = [send(wu.at[:, x, c], wu.at[:, x, c], partner)]
    val2.relay()
    down1.relay()
    key2.relay()
    gate1.finish()
    local_gate.wait()
    gate2.start()
    gate_share = [send(wg.at[y, :, c], wg.at[y, :, c], partner)]
    val2.finish()
    key2.finish()

    bias4 = jnp.concatenate([bias] * 4, axis=0)
    in_group4 = jnp.concatenate([in_group] * 4, axis=0)

    def head(h, carry):
        lanes = pl.ds(pl.multiple_of(h * 256, 256), 256)
        block = q_in[:, lanes].astype(F32) * 0.125
        rows = [part * in_group for b in (0, 1) for part in twice(block[:, 128 * b:128 * b + 128])]
        qx = jnp.concatenate(rows, axis=0).astype(BF16)
        keys = kbuf[:, :, h].reshape(1024, 256)
        contract = (((1,), (1,)), ((), ()))
        s1 = lax.dot_general(qx, keys, contract, preferred_element_type=F32)
        s2 = lax.dot_general(qx, ks[h], contract, preferred_element_type=F32) + bias4
        top = jnp.maximum(
            jnp.max(s1, axis=1, keepdims=True), jnp.max(s2, axis=1, keepdims=True)
        )
        p1, p2 = jnp.exp(s1 - top), jnp.exp(s2 - top)
        total = jnp.sum(p1, axis=1, keepdims=True) + jnp.sum(p2, axis=1, keepdims=True)
        o = jnp.dot(p1.astype(BF16), vbuf[:, :, h].reshape(1024, 256), preferred_element_type=F32)
        o = o + jnp.dot(p2.astype(BF16), vs[h], preferred_element_type=F32)
        o = o * in_group4
        o = o[:, :128] + o[:, 128:]
        o = (o + pltpu.roll(o, 64, 1)) * (1.0 / total)
        left, right = jnp.where(low, o[0:128], o[128:256]), jnp.where(low, o[256:384], o[384:512])
        attn[:, lanes] = jnp.concatenate([left, right], axis=1).astype(BF16)
        return carry

    lax.fori_loop(0, 4, head, 0)

    up2.relay()
    down1.finish()
    local_down.wait()
    down2.start()
    down_share = [send(wd.at[x, c], wd.at[x, c], partner)]
    for i in up2.around()[:2]:
        up_share.append(send(wu.at[:, i, c], wu.at[:, i, c], partner))

    local_out.wait()
    local_res.wait()

    def project(n, square):
        lanes = pl.ds(pl.multiple_of(n * 256, 256), 256)
        part = resb[:, lanes].astype(F32) + jnp.dot(
            attn[...], owb[:, lanes], preferred_element_type=F32
        )
        hid[:, lanes] = part
        return square + jnp.sum(part * part, axis=1, keepdims=True)

    square = lax.fori_loop(0, 8, project, jnp.zeros((128, 1), F32))
    scale = lax.rsqrt(square * (1.0 / 2048) + EPSILON)
    xn[0] = (hid[...] * scale * gain_in[...]).astype(BF16)

    tok_up = send(xn.at[0], xn.at[3], zs[1])
    tok_down = send(xn.at[0], xn.at[1], zs[-1])
    tok_up.wait_recv()
    tok_a = send(xn.at[3, pl.ds(0, 64)], xn.at[2, pl.ds(0, 64)], zs[1])
    tok_down.wait_recv()
    tok_b = send(xn.at[1, pl.ds(64, 64)], xn.at[2, pl.ds(64, 64)], zs[-1])

    gate2.relay()
    for i in gate2.around()[:2]:
        gate_share.append(send(wg.at[i, :, c], wg.at[i, :, c], partner))
    up2.finish()
    i = up2.around()[2]
    up_share.append(send(wu.at[:, i, c], wu.at[:, i, c], partner))
    down2.relay()
    for i in down2.around()[:2]:
        down_share.append(send(wd.at[i, c], wd.at[i, c], partner))
    gate2.finish()
    i = gate2.around()[2]
    gate_share.append(send(wg.at[i, :, c], wg.at[i, :, c], partner))
    tok_a.wait_recv()
    tok_b.wait_recv()
    for copy in up_share + gate_share:
        copy.wait_recv()

    def hidden_units(i, carry):
        block, cols = i // 2, pl.ds(pl.multiple_of(lax.rem(i, 2) * 256, 256), 256)
        tokens = xn[...].reshape(512, 2048)
        g = jnp.dot(tokens, wg[block, :, :, :, cols].reshape(2048, 256), preferred_element_type=F32)
        u = jnp.dot(tokens, wu[block, :, :, :, cols].reshape(2048, 256), preferred_element_type=F32)
        act[:, pl.ds(pl.multiple_of(i * 256, 256), 256)] = (g / (1.0 + jnp.exp(-g)) * u).astype(BF16)
        return carry

    lax.fori_loop(0, 8, hidden_units, 0)

    returns = []

    def down_columns(i):
        for cc in range(2):
            block = i * 2 + cc
            part = jnp.dot(act[...], wd[i, cc].reshape(2048, 256), preferred_element_type=F32)
            acc[block] = part[0:128]
            for k in (1, 2, 3):
                stage[k, block] = part[128 * k:128 * k + 128].astype(BF16)
                target = zs[{1: 1, 2: 2, 3: -1}[k]]
                returns.append(send(stage.at[k, block], back.at[4 - k, block], target))

    down_share[0].wait_recv()
    down_columns(x)
    a, b, far = down2.around()
    down_share[1].wait_recv()
    down_columns(a)
    down_share[2].wait_recv()
    down_columns(b)
    down2.finish()
    down_share.append(send(wd.at[far, c], wd.at[far, c], partner))
    down_share[3].wait_recv()
    down_columns(far)

    for copy in returns:
        copy.wait_recv()
    for n in range(8):
        lanes = slice(256 * n, 256 * n + 256)
        terms = acc[n] + back[1, n].astype(F32) + back[2, n].astype(F32) + back[3, n].astype(F32)
        out[:, lanes] = (hid[:, lanes] + terms).astype(BF16)

    for copy in started:
        copy.wait_send()


def shards(
    residual, queries, keys, values, prefix_keys, cached_prefix_values, out_weight, norm_gain,
    w_gate, w_up, w_down, suffix_lengths, request_group, placement_order,
):
    vmem = pl.BlockSpec(memory_space=pltpu.VMEM)
    anywhere = pl.BlockSpec(memory_space=pl.ANY)
    return pl.pallas_call(
        kernel,
        out_shape=jax.ShapeDtypeStruct((128, 2048), BF16),
        in_specs=[
            anywhere, vmem, vmem, vmem, vmem, vmem, anywhere, vmem,
            anywhere, anywhere, anywhere, vmem, vmem, vmem,
        ],
        out_specs=vmem,
        scratch_shapes=[
            pltpu.VMEM((4, 4, 4, 64, 256), BF16),
            pltpu.VMEM((4, 4, 4, 64, 256), BF16),
            pltpu.VMEM((128, 256), BF16),
            pltpu.VMEM((128, 256), BF16),
            pltpu.VMEM((4, 256, 256), BF16),
            pltpu.VMEM((4, 256, 256), BF16),
            pltpu.VMEM((128, 1024), BF16),
            pltpu.VMEM((1024, 2048), BF16),
            pltpu.VMEM((128, 2048), BF16),
            pltpu.VMEM((128, 2048), F32),
            pltpu.VMEM((4, 128, 2048), BF16),
            pltpu.VMEM((4, 4, 2, 256, 512), BF16),
            pltpu.VMEM((4, 4, 2, 256, 512), BF16),
            pltpu.VMEM((4, 2, 4, 512, 256), BF16),
            pltpu.VMEM((512, 2048), BF16),
            pltpu.VMEM((8, 128, 256), F32),
            pltpu.VMEM((4, 8, 128, 256), BF16),
            pltpu.VMEM((4, 8, 128, 256), BF16),
            pltpu.SemaphoreType.DMA((N_SEM,)),
            pltpu.SemaphoreType.DMA((N_SEM,)),
            pltpu.SemaphoreType.DMA((5,)),
        ],
        compiler_params=pltpu.CompilerParams(
            collective_id=0, has_side_effects=True, vmem_limit_bytes=63 << 20
        ),
    )(
        residual, queries, keys, values, prefix_keys, cached_prefix_values, out_weight,
        norm_gain.reshape(1, -1), w_gate, w_up, w_down,
        suffix_lengths, request_group, placement_order,
    )


def solution(mesh):
    placed = (
        P(("grp", "dev"), None),
        P(("grp", "dev"), None),
        P(("grp", "dev"), None),
        P(("grp", "dev"), None),
        P("grp", "dev", None),
        P("grp", "dev", None),
        P(),
        P(),
        P("grp", "dev"),
        P("grp", "dev"),
        P("dev", "grp"),
        P("grp", None),
        P("grp", None),
        P("grp", None),
    )
    return jax.shard_map(
        shards, mesh=mesh, in_specs=placed, out_specs=P(("grp", "dev"), None), check_vma=False
    )
```

time: 462 us -> 136 us (0.29)
  waiting for transfers between devices: 321 us -> 0 us
  Pallas kernels: 0 us -> 132 us
  matrix products: 55.4 us -> 0 us
  local copies, waits for them, and re-layouts: 37.8 us -> 1.88 us
  other arithmetic: 15.6 us -> 0 us
  starting transfers between devices: 14.3 us -> 0 us
  between operations: 13.8 us -> 0.01 us
    all_gather x7 -> x0, waiting for transfers between devices: 171 us -> none  [the longest x1 68.2 us: shards(): shard_piece = lax.all_gather(normed, 'dev', axis=0, tiled=True)]
    pallas_call x0 -> x1, Pallas kernels: none -> 132 us  [shards(): pl.pallas_call(kernel, out_shape=jax.ShapeDtypeStruct((128, 2048), BF16),...]
    reduce_scatter x1 -> x0, waiting for transfers between devices: 87.2 us -> none  [shards(): lax.psum_scatter(jnp.dot(activation, full_down, preferred_element_type=jn...]
    all_to_all x3 -> x0, waiting for transfers between devices: 59.8 us -> none  [the longest x1 50.7 us: shards(): lax.all_to_all(part_outs, 'dev', split_axis=0, concat_axis=0, tiled=True)]
    dot_general x13 -> x0, matrix products: 55.4 us -> none  [the longest x5 22.8 us: block_partial(): jnp.einsum('nkrm,mkd->nkrd', weights.astype(jnp.bfloat16), heads_of_value...]
    all_to_all x3 -> x0, starting transfers between devices: 13.9 us -> none  [the longest x1 5.45 us: shards(): lax.all_to_all(part_outs, 'dev', split_axis=0, concat_axis=0, tiled=True)]
    reduce_sum x10 -> x0, other arithmetic: 11.8 us -> none  [the longest x5 7.4 us: block_partial(): totals = jnp.sum(weights, axis=-1)]
    dynamic_slice x13 -> x0, local copies, waits for them, and re-layouts: 8.8 us -> none  [the longest x4 5.2 us: owner_block(): lax.dynamic_slice_in_dim(row_queries, first_row, step_rows, 0)]
  transfers between devices with their start and end apart: 11 -> 0, of which waited for: 8 -> 0; matrix products, arithmetic and copies ran while one was open for 18% -> 0% of each run, Pallas kernels for 0% -> 0%
where the time goes in v1:
time: 136 us; the launch traced here: 134 us
  Pallas kernels  132 us (97%)
  local copies, waits for them, and re-layouts  1.88 us (1%)
    pallas_call x1, Pallas kernels, shards(): pl.pallas_call(kernel, out_shape=jax.ShapeDtypeStruct((128, 2048), BF16),...  132 us

profile of v1, /device:TPU:0, one launch (start us, length us, event | category | flops | bytes accessed | tf_op | source)
XLA Modules:
  0.0 133.6 jit_solution(17950720946447378328)
XLA Ops:
  0.0 131.8 %shard_map.136 = bf16[128,2048]{1,0:T(8,128)(2,1)} custom-call(bf16[128,2048]{1,0:T(8,128)(2,1)} %res_in.1, bf16[128,1024]{1,0:T(8,128)(2,1)} %q_in.1, bf16[128,256]{1,0:T(8,128)(2,1)} %k_in.1, bf16[128,256]{1,0:T(8,128)(2,1)} %v_in.1, bf16[4,64,256]{2,1,0:T(8,128)(2,1)} %pk_in.1, bf16[4,64,256]{2,1,0:T(8,128)(2,1)} %pv_in.1, bf16[1024,2048]{1,0:T(8,128)(2,1)} %ow_in.1, ...), custom_call_target="tpu_custom_call" | custom-call | tf_op jit(solution)/shard_map/pallas_call | solution.py:325
  131.8 1.9 %copy.16 = bf16[128,2048]{1,0:T(8,128)(2,1)} copy(bf16[128,2048]{1,0:T(8,128)(2,1)} %shard_map.136) | data formatting | bytes 1048576

commit v2 on v1

v2 whole, which is shorter than its diff:
```python
import jax
import jax.numpy as jnp
from jax import lax
from jax.experimental import pallas as pl
from jax.experimental.pallas import tpu as pltpu
from jax.sharding import PartitionSpec as P

EPSILON = 1e-05
NEG_FILL = -1e30
MESH = pl.DeviceIdType.MESH
F32, BF16 = jnp.float32, jnp.bfloat16
N_SEM = 136


def token_info(lengths, groups, order, first_row):
    n = lengths.shape[1]
    rows = lax.broadcasted_iota(jnp.int32, (n, n), 0)
    cols = lax.broadcasted_iota(jnp.int32, (n, n), 1)
    diagonal = rows == cols

    def column(row):
        spread = jnp.broadcast_to(row, (n, n))
        return jnp.sum(jnp.where(diagonal, spread, 0.0), axis=1, keepdims=True)

    picked = jnp.broadcast_to(order, (n, n)) == rows
    packed_len = jnp.sum(jnp.where(picked, column(lengths), 0.0), axis=0, keepdims=True)
    packed_group = jnp.sum(jnp.where(picked, column(groups), 0.0), axis=0, keepdims=True)
    ends = jnp.sum(jnp.where(rows <= cols, column(packed_len), 0.0), axis=0, keepdims=True)
    starts = ends - packed_len
    token = (lax.broadcasted_iota(jnp.int32, (128, n), 0) + first_row).astype(F32)
    inside = (token >= starts) & (token < ends)
    group = jnp.sum(jnp.where(inside, packed_group, 0.0), axis=1, keepdims=True)
    start = jnp.sum(jnp.where(inside, starts, 0.0), axis=1, keepdims=True)
    return group, start


def kernel(
    res_in, q_in, k_in, v_in, pk_in, pv_in, ow_in, gain_in, wg_in, wu_in, wd_in, len_in, grp_in, ord_in,
    out,
    kbuf, vbuf, zk, zv, sk, sv, kprev, vprev, ks, vs, attn, owb, res, hid, xn, wg, wu, wda, wdb, upv, act,
    acc, ends, far, hop, near, back,
    ssem, rsem, lsem,
):
    gi, di = lax.axis_index("grp"), lax.axis_index("dev")
    x, c = gi // 2, lax.rem(gi, 2)
    z, y = di // 4, lax.rem(di, 4)

    def at(xx, cc, zz, yy):
        return (lax.rem(xx + 4, 4) * 2 + cc, lax.rem(zz + 4, 4) * 4 + lax.rem(yy + 4, 4))

    xs = {k: at(x + k, c, z, y) for k in (1, -1)}
    ys = {k: at(x, c, z, y + k) for k in (1, -1)}
    zs = {k: at(x, c, z + k, y) for k in (1, -1)}
    partner = (x * 2 + (1 - c), di)
    peers = [xs[1], xs[-1], ys[1], ys[-1], zs[1], zs[-1], partner]

    barrier = pltpu.get_barrier_semaphore()
    for peer in peers:
        pl.semaphore_signal(barrier, inc=1, device_id=peer, device_id_type=MESH)

    started = []
    counter = [0]

    def send(src, dst, device):
        i = counter[0]
        counter[0] += 1
        copy = pltpu.make_async_remote_copy(
            src_ref=src, dst_ref=dst, send_sem=ssem.at[i], recv_sem=rsem.at[i],
            device_id=device, device_id_type=MESH,
        )
        copy.start()
        started.append(copy)
        return copy

    local_count = [0]

    def bring(src, dst):
        i = local_count[0]
        local_count[0] += 1
        copy = pltpu.make_async_copy(src, dst, lsem.at[i])
        copy.start()
        return copy

    class Ring:
        def __init__(self, where, pos, slot, half):
            self.where, self.pos, self.slot, self.half = where, pos, slot, half

        def start(self, src=None):
            mine = self.slot(self.pos)
            src = mine if src is None else src
            self.up = send(src, mine, self.where[1])
            self.down = send(src, mine, self.where[-1])

        def relay(self):
            before, after = lax.rem(self.pos + 3, 4), lax.rem(self.pos + 1, 4)
            self.up.wait_recv()
            self.a = send(self.half(before, 0), self.half(before, 0), self.where[1])
            self.down.wait_recv()
            self.b = send(self.half(after, 1), self.half(after, 1), self.where[-1])

        def finish(self):
            self.a.wait_recv()
            self.b.wait_recv()

        def around(self):
            return [lax.rem(self.pos + k, 4) for k in (3, 1, 2)]

    class Piece:
        def __init__(self, first, second, src, local):
            self.first, self.second, self.src, self.local = first, second, src, local
            self.shared = []

        def share(self, i):
            block = self.second.slot(i)
            self.shared.append(send(block, block, partner))

        def start(self):
            self.first.start(self.src)

        def relay1(self):
            self.first.relay()

        def finish1(self):
            self.first.finish()
            if self.local is not None:
                self.local.wait()
            self.share(self.second.pos)

        def turn(self):
            self.second.start()

        def relay2(self):
            self.second.relay()
            for i in self.second.around()[:2]:
                self.share(i)

        def finish2(self):
            self.second.finish()
            self.share(self.second.around()[2])

        def ready(self, n=None):
            for copy in self.shared[:n] if n is not None else self.shared:
                copy.wait_recv()
            self.shared = self.shared[n:] if n is not None else []

    local_gate = bring(wg_in, wg.at[y, x, c])
    local_up = bring(wu_in, wu.at[y, x, c])
    local_da = bring(wd_in.at[:, pl.ds(0, 128)], wda.at[c, x, y])
    local_db = bring(wd_in.at[:, pl.ds(128, 128)], wdb.at[c, x, y])
    local_res = bring(res_in, res.at[0])
    local_out = bring(ow_in, owb)

    top, bottom = pl.ds(0, 128), pl.ds(128, 128)

    def quarter(lo, h):
        return pl.ds(lo + 64 * h, 64)

    gate_a = Piece(
        Ring(xs, x, lambda i: wg.at[y, i, c, top], lambda i, h: wg.at[y, i, c, quarter(0, h)]),
        Ring(ys, y, lambda i: wg.at[i, :, c, top], lambda i, h: wg.at[i, pl.ds(2 * h, 2), c, top]),
        wg_in.at[top], local_gate,
    )
    gate_b = Piece(
        Ring(ys, y, lambda i: wg.at[i, x, c, bottom], lambda i, h: wg.at[i, x, c, quarter(128, h)]),
        Ring(xs, x, lambda i: wg.at[:, i, c, bottom], lambda i, h: wg.at[pl.ds(2 * h, 2), i, c, bottom]),
        wg_in.at[bottom], None,
    )
    up_a = Piece(
        Ring(ys, y, lambda i: wu.at[i, x, c, top], lambda i, h: wu.at[i, x, c, quarter(0, h)]),
        Ring(xs, x, lambda i: wu.at[:, i, c, top], lambda i, h: wu.at[pl.ds(2 * h, 2), i, c, top]),
        wu_in.at[top], local_up,
    )
    up_b = Piece(
        Ring(ys, y, lambda i: wu.at[i, x, c, bottom], lambda i, h: wu.at[i, x, c, quarter(128, h)]),
        Ring(xs, x, lambda i: wu.at[:, i, c, bottom], lambda i, h: wu.at[pl.ds(2 * h, 2), i, c, bottom]),
        wu_in.at[bottom], None,
    )
    down_a = Piece(
        Ring(xs, x, lambda i: wda.at[c, i, y], lambda i, h: wda.at[c, i, y, pl.ds(256 * h, 256)]),
        Ring(ys, y, lambda i: wda.at[c, :, i], lambda i, h: wda.at[c, pl.ds(2 * h, 2), i]),
        wd_in.at[:, pl.ds(0, 128)], local_da,
    )
    down_b = Piece(
        Ring(ys, y, lambda i: wdb.at[c, x, i], lambda i, h: wdb.at[c, x, i, pl.ds(256 * h, 256)]),
        Ring(xs, x, lambda i: wdb.at[c, i], lambda i, h: wdb.at[c, i, pl.ds(2 * h, 2)]),
        wd_in.at[:, pl.ds(128, 128)], local_db,
    )
    key1 = Ring(ys, y, lambda i: kbuf.at[z, i], lambda i, h: kbuf.at[z, i, pl.ds(2 * h, 2)])
    key2 = Ring(zs, z, lambda i: kbuf.at[i], lambda i, h: kbuf.at[i, pl.ds(2 * h, 2)])
    val1 = Ring(zs, z, lambda i: vbuf.at[i, y], lambda i, h: vbuf.at[i, y, pl.ds(2 * h, 2)])
    val2 = Ring(ys, y, lambda i: vbuf.at[:, i], lambda i, h: vbuf.at[pl.ds(2 * h, 2), i])

    low64 = lax.broadcasted_iota(jnp.int32, (64, 128), 1) < 64
    for src, dst in ((pk_in, kbuf), (pv_in, vbuf)):
        for h in range(4):
            cut = slice(128 * (h // 2), 128 * (h // 2) + 128)
            pairs = []
            for g in (0, 2):
                a, b = src[g, :, cut].astype(F32), src[g + 1, :, cut].astype(F32)
                if h % 2 == 0:
                    pairs.append(jnp.where(low64, a, pltpu.roll(b, 64, 1)))
                else:
                    pairs.append(jnp.where(low64, pltpu.roll(a, 64, 1), b))
            dst[z, y, h] = jnp.concatenate(pairs, axis=1).astype(BF16)

    pl.semaphore_wait(barrier, len(peers))
    key1.start()
    val1.start()
    gate_a.start()
    up_a.start()
    up_b.start()
    down_a.start()
    over_k = send(k_in, zk, zs[1])
    over_v = send(v_in, zv, zs[1])

    first_row = di * 128
    group, start = token_info(
        len_in[...].astype(F32), grp_in[...].astype(F32), ord_in[...], first_row
    )
    lane_group = (lax.broadcasted_iota(jnp.int32, (128, 256), 1) // 64).astype(F32)
    in_group = (lane_group == group).astype(F32)
    window = (lax.broadcasted_iota(jnp.int32, (128, 256), 1) + (first_row - 128)).astype(F32)
    token = (lax.broadcasted_iota(jnp.int32, (128, 256), 0) + first_row).astype(F32)
    bias = jnp.where((window >= start) & (window <= token), 0.0, NEG_FILL)
    low = lax.broadcasted_iota(jnp.int32, (128, 128), 1) < 64

    def twice(block):
        turned = pltpu.roll(block, 64, 1)
        first, second = jnp.where(low, block, turned), jnp.where(low, turned, block)
        return jnp.concatenate([first, first], axis=1), jnp.concatenate([second, second], axis=1)

    def spread(src, dst, row):
        for b in (0, 1):
            first, second = twice(src[:, 128 * b:128 * b + 128].astype(F32))
            dst[2 * b, row:row + 128] = first.astype(BF16)
            dst[2 * b + 1, row:row + 128] = second.astype(BF16)

    key1.relay()
    val1.relay()
    up_a.relay1()
    up_b.relay1()
    gate_a.relay1()
    val1.finish()
    val2.start()
    key1.finish()
    key2.start()
    gate_b.start()
    up_a.finish1()
    up_a.turn()
    up_b.finish1()
    up_b.turn()
    down_a.relay1()

    over_k.wait_recv()
    over_v.wait_recv()
    edge = (y == 3).astype(F32)
    for src, over, staged in ((k_in, zk, sk), (v_in, zv, sv)):
        staged[...] = (
            over[...].astype(F32) * edge + src[...].astype(F32) * (1.0 - edge)
        ).astype(BF16)
    next_k = send(sk, kprev, ys[1])
    next_v = send(sv, vprev, ys[1])
    spread(k_in, ks, 128)
    spread(v_in, vs, 128)

    gate_a.finish1()
    down_a.finish1()
    key2.relay()
    val2.relay()
    down_b.start()
    gate_b.relay1()
    local_res.wait()
    tokens_up = send(res.at[0], res.at[3], zs[1])
    tokens_down = send(res.at[0], res.at[1], zs[-1])
    next_k.wait_recv()
    next_v.wait_recv()
    spread(kprev, ks, 0)
    spread(vprev, vs, 0)
    up_a.relay2()
    gate_a.turn()
    key2.finish()
    val2.finish()

    bias4 = jnp.concatenate([bias] * 4, axis=0)
    in_group4 = jnp.concatenate([in_group] * 4, axis=0)

    def head(h):
        lanes = slice(256 * h, 256 * h + 256)
        block = q_in[:, lanes].astype(F32) * 0.125
        rows = [part * in_group for b in (0, 1) for part in twice(block[:, 128 * b:128 * b + 128])]
        qx = jnp.concatenate(rows, axis=0).astype(BF16)
        keys = kbuf[:, :, h].reshape(1024, 256)
        contract = (((1,), (1,)), ((), ()))
        s1 = lax.dot_general(qx, keys, contract, preferred_element_type=F32)
        s2 = lax.dot_general(qx, ks[h], contract, preferred_element_type=F32) + bias4
        peak = jnp.maximum(
            jnp.max(s1, axis=1, keepdims=True), jnp.max(s2, axis=1, keepdims=True)
        )
        p1, p2 = jnp.exp(s1 - peak), jnp.exp(s2 - peak)
        total = jnp.sum(p1, axis=1, keepdims=True) + jnp.sum(p2, axis=1, keepdims=True)
        o = jnp.dot(p1.astype(BF16), vbuf[:, :, h].reshape(1024, 256), preferred_element_type=F32)
        o = o + jnp.dot(p2.astype(BF16), vs[h], preferred_element_type=F32)
        o = o * in_group4
        o = o[:, :128] + o[:, 128:]
        o = (o + pltpu.roll(o, 64, 1)) * (1.0 / total)
        left, right = jnp.where(low, o[0:128], o[128:256]), jnp.where(low, o[256:384], o[384:512])
        attn[0, :, lanes] = jnp.concatenate([left, right], axis=1).astype(BF16)

    def pair_start(p):
        lanes = pl.ds(512 * p, 512)
        return [
            send(attn.at[0, :, lanes], attn.at[3, :, lanes], zs[1]),
            send(attn.at[0, :, lanes], attn.at[1, :, lanes], zs[-1]),
        ]

    def onward(buf, copies, lanes):
        copies[0].wait_recv()
        a = send(buf.at[3, pl.ds(0, 64), lanes], buf.at[2, pl.ds(0, 64), lanes], zs[1])
        copies[1].wait_recv()
        b = send(buf.at[1, pl.ds(64, 64), lanes], buf.at[2, pl.ds(64, 64), lanes], zs[-1])
        return [a, b]

    head(0)
    head(1)
    pair0 = pair_start(0)
    up_b.relay2()
    gate_b.finish1()
    gate_b.turn()
    head(2)
    res_far = onward(res, [tokens_up, tokens_down], pl.ds(0, 2048))
    head(3)
    pair1 = pair_start(1)
    pair0 = onward(attn, pair0, pl.ds(0, 512))
    down_b.relay1()
    up_a.finish2()
    pair1 = onward(attn, pair1, pl.ds(512, 512))
    up_b.finish2()
    for copy in res_far + pair0 + pair1:
        copy.wait_recv()
    local_out.wait()

    def project(n, square):
        lanes = pl.ds(pl.multiple_of(n * 256, 256), 256)
        part = res[:, :, lanes].reshape(512, 256).astype(F32) + jnp.dot(
            attn[...].reshape(512, 1024), owb[:, lanes], preferred_element_type=F32
        )
        hid[:, lanes] = part
        return square + jnp.sum(part * part, axis=1, keepdims=True)

    square = lax.fori_loop(0, 8, project, jnp.zeros((512, 1), F32))
    scale = lax.rsqrt(square * (1.0 / 2048) + EPSILON)

    def normalize(n, carry):
        lanes = pl.ds(pl.multiple_of(n * 256, 256), 256)
        xn[:, lanes] = (hid[:, lanes] * scale * gain_in[:, lanes]).astype(BF16)
        return carry

    lax.fori_loop(0, 8, normalize, 0)

    up_a.ready()
    up_b.ready()

    def up_units(i, carry):
        block, cols = i // 2, pl.ds(pl.multiple_of(lax.rem(i, 2) * 256, 256), 256)
        upv[i] = jnp.dot(
            xn[...], wu[block, :, :, :, cols].reshape(2048, 256), preferred_element_type=F32
        )
        return carry

    lax.fori_loop(0, 4, up_units, 0)
    gate_a.relay2()
    down_a.turn()
    down_b.finish1()
    lax.fori_loop(4, 8, up_units, 0)
    gate_b.relay2()
    down_b.turn()
    gate_a.finish2()
    gate_b.finish2()
    gate_a.ready()
    gate_b.ready()

    def gate_units(i, carry):
        block, cols = i // 2, pl.ds(pl.multiple_of(lax.rem(i, 2) * 256, 256), 256)
        g = jnp.dot(
            xn[...], wg[block, :, :, :, cols].reshape(2048, 256), preferred_element_type=F32
        )
        act[:, pl.ds(pl.multiple_of(i * 256, 256), 256)] = (
            g / (1.0 + jnp.exp(-g)) * upv[i]
        ).astype(BF16)
        return carry

    lax.fori_loop(0, 8, gate_units, 0)

    half0, half1 = pl.ds(0, 64), pl.ds(64, 64)
    hops, returns = {}, []

    def block_sums(half, i):
        weight = (wda, wdb)[half]
        part = jnp.dot(
            act[...],
            jnp.concatenate([weight[0, i].reshape(2048, 128), weight[1, i].reshape(2048, 128)], axis=1),
            preferred_element_type=F32,
        )
        n = half * 4 + i
        acc[n] = part[0:128]
        ends[0, n] = part[128:256]
        ends[1, n] = part[384:512]
        far[n] = part[256:384].astype(BF16)
        hops[len(hops)] = (
            n,
            send(far.at[n, half0], hop.at[0, n], zs[1]),
            send(far.at[n, half1], hop.at[1, n], zs[-1]),
        )

    def pass_on(k):
        n, a, b = hops[k]
        a.wait_recv()
        near[0, n, 0:64] = (ends[0, n, 0:64] + hop[0, n].astype(F32)).astype(BF16)
        near[0, n, 64:128] = ends[0, n, 64:128].astype(BF16)
        returns.append(send(near.at[0, n], back.at[0, n], zs[1]))
        b.wait_recv()
        near[1, n, 0:64] = ends[1, n, 0:64].astype(BF16)
        near[1, n, 64:128] = (ends[1, n, 64:128] + hop[1, n].astype(F32)).astype(BF16)
        returns.append(send(near.at[1, n], back.at[1, n], zs[-1]))

    before, after, opposite = [lax.rem(x + k, 4) for k in (3, 1, 2)]
    down_b.ready(1)
    block_sums(1, x)
    down_b.relay2()
    down_a.relay2()
    down_b.ready(2)
    block_sums(1, before)
    pass_on(0)
    block_sums(1, after)
    pass_on(1)
    down_a.finish2()
    down_a.ready()
    for step, i in enumerate((x, before, after, opposite)):
        block_sums(0, i)
        pass_on(2 + step)
    down_b.finish2()
    down_b.ready()
    block_sums(1, opposite)
    pass_on(6)
    pass_on(7)

    for copy in returns:
        copy.wait_recv()
    for half in range(2):
        for i in range(4):
            n = half * 4 + i
            total = acc[n] + back[0, n].astype(F32) + back[1, n].astype(F32)
            for cc in range(2):
                lanes = slice(512 * i + 256 * cc + 128 * half, 512 * i + 256 * cc + 128 * half + 128)
                out[:, lanes] = (hid[0:128, lanes] + total[:, 128 * cc:128 * cc + 128]).astype(BF16)

    for copy in started:
        copy.wait_send()
    assert counter[0] == N_SEM, counter[0]


def shards(
    residual, queries, keys, values, prefix_keys, cached_prefix_values, out_weight, norm_gain,
    w_gate, w_up, w_down, suffix_lengths, request_group, placement_order,
):
    vmem = pl.BlockSpec(memory_space=pltpu.VMEM)
    anywhere = pl.BlockSpec(memory_space=pl.ANY)
    return pl.pallas_call(
        kernel,
        out_shape=jax.ShapeDtypeStruct((128, 2048), BF16),
        in_specs=[
            anywhere, vmem, vmem, vmem, vmem, vmem, anywhere, vmem,
            anywhere, anywhere, anywhere, vmem, vmem, vmem,
        ],
        out_specs=vmem,
        scratch_shapes=[
            pltpu.VMEM((4, 4, 4, 64, 256), BF16),
            pltpu.VMEM((4, 4, 4, 64, 256), BF16),
            pltpu.VMEM((128, 256), BF16),
            pltpu.VMEM((128, 256), BF16),
            pltpu.VMEM((128, 256), BF16),
            pltpu.VMEM((128, 256), BF16),
            pltpu.VMEM((128, 256), BF16),
            pltpu.VMEM((128, 256), BF16),
            pltpu.VMEM((4, 256, 256), BF16),
            pltpu.VMEM((4, 256, 256), BF16),
            pltpu.VMEM((4, 128, 1024), BF16),
            pltpu.VMEM((1024, 2048), BF16),
            pltpu.VMEM((4, 128, 2048), BF16),
            pltpu.VMEM((512, 2048), F32),
            pltpu.VMEM((512, 2048), BF16),
            pltpu.VMEM((4, 4, 2, 256, 512), BF16),
            pltpu.VMEM((4, 4, 2, 256, 512), BF16),
            pltpu.VMEM((2, 4, 4, 512, 128), BF16),
            pltpu.VMEM((2, 4, 4, 512, 128), BF16),
            pltpu.VMEM((8, 512, 256), F32),
            pltpu.VMEM((512, 2048), BF16),
            pltpu.VMEM((8, 128, 256), F32),
            pltpu.VMEM((2, 8, 128, 256), F32),
            pltpu.VMEM((8, 128, 256), BF16),
            pltpu.VMEM((2, 8, 64, 256), BF16),
            pltpu.VMEM((2, 8, 128, 256), BF16),
            pltpu.VMEM((2, 8, 128, 256), BF16),
            pltpu.SemaphoreType.DMA((N_SEM,)),
            pltpu.SemaphoreType.DMA((N_SEM,)),
            pltpu.SemaphoreType.DMA((6,)),
        ],
        compiler_params=pltpu.CompilerParams(
            collective_id=0, has_side_effects=True, vmem_limit_bytes=63 << 20
        ),
    )(
        residual, queries, keys, values, prefix_keys, cached_prefix_values, out_weight,
        norm_gain.reshape(1, -1), w_gate, w_up, w_down,
        suffix_lengths, request_group, placement_order,
    )


def solution(mesh):
    placed = (
        P(("grp", "dev"), None),
        P(("grp", "dev"), None),
        P(("grp", "dev"), None),
        P(("grp", "dev"), None),
        P("grp", "dev", None),
        P("grp", "dev", None),
        P(),
        P(),
        P("grp", "dev"),
        P("grp", "dev"),
        P("dev", "grp"),
        P("grp", None),
        P("grp", None),
        P("grp", None),
    )
    return jax.shard_map(
        shards, mesh=mesh, in_specs=placed, out_specs=P(("grp", "dev"), None), check_vma=False
    )
```

time: 136 us -> 142 us (1.044); the launches traced: 134 us -> 142 us
  Pallas kernels: 132 us -> 140 us
    pallas_call x1, Pallas kernels: 132 us -> 140 us  [shards(): pl.pallas_call(kernel, out_shape=jax.ShapeDtypeStruct((128, 2048), BF16),...]
where the time goes in v2:
time: 142 us
  Pallas kernels  140 us (99%)
  local copies, waits for them, and re-layouts  1.88 us (1%)
    pallas_call x1, Pallas kernels, shards(): pl.pallas_call(kernel, out_shape=jax.ShapeDtypeStruct((128, 2048), BF16),...  140 us

profile of v2, /device:TPU:0, one launch (start us, length us, event | category | flops | bytes accessed | tf_op | source)
XLA Modules:
  0.0 142.1 jit_solution(14576401578324554245)
XLA Ops:
  0.0 140.2 %shard_map.136 = bf16[128,2048]{1,0:T(8,128)(2,1)} custom-call(bf16[128,2048]{1,0:T(8,128)(2,1)} %res_in.1, bf16[128,1024]{1,0:T(8,128)(2,1)} %q_in.1, bf16[128,256]{1,0:T(8,128)(2,1)} %k_in.1, bf16[128,256]{1,0:T(8,128)(2,1)} %v_in.1, bf16[4,64,256]{2,1,0:T(8,128)(2,1)} %pk_in.1, bf16[4,64,256]{2,1,0:T(8,128)(2,1)} %pv_in.1, bf16[1024,2048]{1,0:T(8,128)(2,1)} %ow_in.1, ...), custom_call_target="tpu_custom_call" | custom-call | tf_op jit(solution)/shard_map/pallas_call | solution.py:468
  140.2 1.9 %copy.16 = bf16[128,2048]{1,0:T(8,128)(2,1)} copy(bf16[128,2048]{1,0:T(8,128)(2,1)} %shard_map.136) | data formatting | bytes 1048576

commit v3 on v2

--- a/solution.py
+++ b/solution.py
@@ -9,7 +9,7 @@
 NEG_FILL = -1e30
 MESH = pl.DeviceIdType.MESH
 F32, BF16 = jnp.float32, jnp.bfloat16
-N_SEM = 136
+N_SEM = 164
 
 
 def token_info(lengths, groups, order, first_row):
@@ -37,7 +37,7 @@
 def kernel(
     res_in, q_in, k_in, v_in, pk_in, pv_in, ow_in, gain_in, wg_in, wu_in, wd_in, len_in, grp_in, ord_in,
     out,
-    kbuf, vbuf, zk, zv, sk, sv, kprev, vprev, ks, vs, attn, owb, res, hid, xn, wg, wu, wda, wdb, upv, act,
+    kbuf, vbuf, zk, zv, sk, sv, kprev, vprev, ks, vs, attn, owb, res, hid, xn, wg, wu, wd, upv, act,
     acc, ends, far, hop, near, back,
     ssem, rsem, lsem,
 ):
@@ -61,13 +61,29 @@
     started = []
     counter = [0]
 
+    class Copy:
+        def __init__(self, src, dst, device, i):
+            self.src, self.dst, self.device, self.i = src, dst, device, i
+
+        def copy(self):
+            src, dst = [ref() if callable(ref) else ref for ref in (self.src, self.dst)]
+            return pltpu.make_async_remote_copy(
+                src_ref=src, dst_ref=dst, send_sem=ssem.at[self.i], recv_sem=rsem.at[self.i],
+                device_id=self.device, device_id_type=MESH,
+            )
+
+        def start(self):
+            self.copy().start()
+
+        def wait_recv(self):
+            self.copy().wait_recv()
+
+        def wait_send(self):
+            self.copy().wait_send()
+
     def send(src, dst, device):
-        i = counter[0]
+        copy = Copy(src, dst, device, counter[0])
         counter[0] += 1
-        copy = pltpu.make_async_remote_copy(
-            src_ref=src, dst_ref=dst, send_sem=ssem.at[i], recv_sem=rsem.at[i],
-            device_id=device, device_id_type=MESH,
-        )
         copy.start()
         started.append(copy)
         return copy
@@ -84,26 +100,28 @@
     class Ring:
         def __init__(self, where, pos, slot, half):
             self.where, self.pos, self.slot, self.half = where, pos, slot, half
+            self.before, self.after, self.far = [lax.rem(pos + k, 4) for k in (3, 1, 2)]
 
         def start(self, src=None):
-            mine = self.slot(self.pos)
+            mine = lambda: self.slot(self.pos)
             src = mine if src is None else src
             self.up = send(src, mine, self.where[1])
             self.down = send(src, mine, self.where[-1])
 
         def relay(self):
-            before, after = lax.rem(self.pos + 3, 4), lax.rem(self.pos + 1, 4)
+            before, after = self.before, self.after
             self.up.wait_recv()
-            self.a = send(self.half(before, 0), self.half(before, 0), self.where[1])
+            first, second = lambda: self.half(before, 0), lambda: self.half(after, 1)
+            self.a = send(first, first, self.where[1])
             self.down.wait_recv()
-            self.b = send(self.half(after, 1), self.half(after, 1), self.where[-1])
+            self.b = send(second, second, self.where[-1])
 
         def finish(self):
             self.a.wait_recv()
             self.b.wait_recv()
 
         def around(self):
-            return [lax.rem(self.pos + k, 4) for k in (3, 1, 2)]
+            return [self.before, self.after, self.far]
 
     class Piece:
         def __init__(self, first, second, src, local):
@@ -111,7 +129,7 @@
             self.shared = []
 
         def share(self, i):
-            block = self.second.slot(i)
+            block = lambda: self.second.slot(i)
             self.shared.append(send(block, block, partner))
 
         def start(self):
@@ -145,8 +163,8 @@
 
     local_gate = bring(wg_in, wg.at[y, x, c])
     local_up = bring(wu_in, wu.at[y, x, c])
-    local_da = bring(wd_in.at[:, pl.ds(0, 128)], wda.at[c, x, y])
-    local_db = bring(wd_in.at[:, pl.ds(128, 128)], wdb.at[c, x, y])
+    local_da = bring(wd_in.at[:, pl.ds(0, 128)], wd.at[0, c, x, y])
+    local_db = bring(wd_in.at[:, pl.ds(128, 128)], wd.at[1, c, x, y])
     local_res = bring(res_in, res.at[0])
     local_out = bring(ow_in, owb)
 
@@ -176,19 +194,28 @@
         wu_in.at[bottom], None,
     )
     down_a = Piece(
-        Ring(xs, x, lambda i: wda.at[c, i, y], lambda i, h: wda.at[c, i, y, pl.ds(256 * h, 256)]),
-        Ring(ys, y, lambda i: wda.at[c, :, i], lambda i, h: wda.at[c, pl.ds(2 * h, 2), i]),
+        Ring(xs, x, lambda i: wd.at[0, c, i, y], lambda i, h: wd.at[0, c, i, y, pl.ds(256 * h, 256)]),
+        Ring(ys, y, lambda i: wd.at[0, c, :, i], lambda i, h: wd.at[0, c, pl.ds(2 * h, 2), i]),
         wd_in.at[:, pl.ds(0, 128)], local_da,
     )
     down_b = Piece(
-        Ring(ys, y, lambda i: wdb.at[c, x, i], lambda i, h: wdb.at[c, x, i, pl.ds(256 * h, 256)]),
-        Ring(xs, x, lambda i: wdb.at[c, i], lambda i, h: wdb.at[c, i, pl.ds(2 * h, 2)]),
+        Ring(ys, y, lambda i: wd.at[1, c, x, i], lambda i, h: wd.at[1, c, x, i, pl.ds(256 * h, 256)]),
+        Ring(xs, x, lambda i: wd.at[1, c, i], lambda i, h: wd.at[1, c, i, pl.ds(2 * h, 2)]),
         wd_in.at[:, pl.ds(128, 128)], local_db,
     )
     key1 = Ring(ys, y, lambda i: kbuf.at[z, i], lambda i, h: kbuf.at[z, i, pl.ds(2 * h, 2)])
-    key2 = Ring(zs, z, lambda i: kbuf.at[i], lambda i, h: kbuf.at[i, pl.ds(2 * h, 2)])
     val1 = Ring(zs, z, lambda i: vbuf.at[i, y], lambda i, h: vbuf.at[i, y, pl.ds(2 * h, 2)])
-    val2 = Ring(ys, y, lambda i: vbuf.at[:, i], lambda i, h: vbuf.at[pl.ds(2 * h, 2), i])
+
+    def pair_rings(heads):
+        key = Ring(
+            zs, z, lambda i: kbuf.at[i, :, heads], lambda i, h: kbuf.at[i, pl.ds(2 * h, 2), heads]
+        )
+        val = Ring(
+            ys, y, lambda i: vbuf.at[:, i, heads], lambda i, h: vbuf.at[pl.ds(2 * h, 2), i, heads]
+        )
+        return key, val
+
+    (key2a, val2a), (key2b, val2b) = pair_rings(pl.ds(0, 2)), pair_rings(pl.ds(2, 2))
 
     low64 = lax.broadcasted_iota(jnp.int32, (64, 128), 1) < 64
     for src, dst in ((pk_in, kbuf), (pv_in, vbuf)):
@@ -208,7 +235,6 @@
     val1.start()
     gate_a.start()
     up_a.start()
-    up_b.start()
     down_a.start()
     over_k = send(k_in, zk, zs[1])
     over_v = send(v_in, zv, zs[1])
@@ -238,18 +264,7 @@
     key1.relay()
     val1.relay()
     up_a.relay1()
-    up_b.relay1()
-    gate_a.relay1()
-    val1.finish()
-    val2.start()
-    key1.finish()
-    key2.start()
-    gate_b.start()
-    up_a.finish1()
-    up_a.turn()
-    up_b.finish1()
-    up_b.turn()
-    down_a.relay1()
+    up_b.start()
 
     over_k.wait_recv()
     over_v.wait_recv()
@@ -260,26 +275,55 @@
         ).astype(BF16)
     next_k = send(sk, kprev, ys[1])
     next_v = send(sv, vprev, ys[1])
+
+    gate_a.relay1()
+    down_a.relay1()
+    key1.finish()
+    key2a.start()
+    key2b.start()
+    up_a.finish1()
+    up_a.turn()
+    up_b.relay1()
+    val1.finish()
+    val2a.start()
+    val2b.start()
+
+    def spread_z(buf, lanes):
+        return [
+            send(buf.at[0, :, lanes], buf.at[3, :, lanes], zs[1]),
+            send(buf.at[0, :, lanes], buf.at[1, :, lanes], zs[-1]),
+        ]
+
+    def onward(buf, copies, lanes):
+        copies[0].wait_recv()
+        a = send(buf.at[3, pl.ds(0, 64), lanes], buf.at[2, pl.ds(0, 64), lanes], zs[1])
+        copies[1].wait_recv()
+        b = send(buf.at[1, pl.ds(64, 64), lanes], buf.at[2, pl.ds(64, 64), lanes], zs[-1])
+        return [a, b]
+
+    res_lanes = [pl.ds(512 * n, 512) for n in range(4)]
+    head_lanes = [pl.ds(256 * n, 256) for n in range(4)]
+    local_res.wait()
+    res_copies = [spread_z(res, res_lanes[0])]
     spread(k_in, ks, 128)
     spread(v_in, vs, 128)
-
+    key2a.relay()
+    up_b.finish1()
+    up_b.turn()
     gate_a.finish1()
-    down_a.finish1()
-    key2.relay()
-    val2.relay()
+    key2b.relay()
+    res_copies += [spread_z(res, lanes) for lanes in res_lanes[1:]]
+    val2a.relay()
+    up_a.relay2()
+    val2b.relay()
+    gate_b.start()
     down_b.start()
-    gate_b.relay1()
-    local_res.wait()
-    tokens_up = send(res.at[0], res.at[3], zs[1])
-    tokens_down = send(res.at[0], res.at[1], zs[-1])
     next_k.wait_recv()
     next_v.wait_recv()
     spread(kprev, ks, 0)
     spread(vprev, vs, 0)
-    up_a.relay2()
-    gate_a.turn()
-    key2.finish()
-    val2.finish()
+    key2a.finish()
+    val2a.finish()
 
     bias4 = jnp.concatenate([bias] * 4, axis=0)
     in_group4 = jnp.concatenate([in_group] * 4, axis=0)
@@ -306,153 +350,193 @@
         left, right = jnp.where(low, o[0:128], o[128:256]), jnp.where(low, o[256:384], o[384:512])
         attn[0, :, lanes] = jnp.concatenate([left, right], axis=1).astype(BF16)
 
-    def pair_start(p):
-        lanes = pl.ds(512 * p, 512)
-        return [
-            send(attn.at[0, :, lanes], attn.at[3, :, lanes], zs[1]),
-            send(attn.at[0, :, lanes], attn.at[1, :, lanes], zs[-1]),
-        ]
-
-    def onward(buf, copies, lanes):
-        copies[0].wait_recv()
-        a = send(buf.at[3, pl.ds(0, 64), lanes], buf.at[2, pl.ds(0, 64), lanes], zs[1])
-        copies[1].wait_recv()
-        b = send(buf.at[1, pl.ds(64, 64), lanes], buf.at[2, pl.ds(64, 64), lanes], zs[-1])
-        return [a, b]
-
     head(0)
+    attn_copies = [spread_z(attn, head_lanes[0])]
+    key2b.finish()
+    val2b.finish()
     head(1)
-    pair0 = pair_start(0)
+    attn_copies.append(spread_z(attn, head_lanes[1]))
     up_b.relay2()
+    arriving = [onward(res, res_copies[0], res_lanes[0])]
+    arriving.append(onward(res, res_copies[1], res_lanes[1]))
+    gate_b.relay1()
+    gate_a.turn()
+    head(2)
+    attn_copies.append(spread_z(attn, head_lanes[2]))
+    down_b.relay1()
+    arriving.append(onward(attn, attn_copies[0], head_lanes[0]))
     gate_b.finish1()
     gate_b.turn()
-    head(2)
-    res_far = onward(res, [tokens_up, tokens_down], pl.ds(0, 2048))
     head(3)
-    pair1 = pair_start(1)
-    pair0 = onward(attn, pair0, pl.ds(0, 512))
-    down_b.relay1()
+    attn_copies.append(spread_z(attn, head_lanes[3]))
+    arriving.append(onward(attn, attn_copies[1], head_lanes[1]))
+    arriving.append(onward(res, res_copies[2], res_lanes[2]))
+    arriving.append(onward(res, res_copies[3], res_lanes[3]))
+    arriving.append(onward(attn, attn_copies[2], head_lanes[2]))
     up_a.finish2()
-    pair1 = onward(attn, pair1, pl.ds(512, 512))
+    down_a.finish1()
+    last = onward(attn, attn_copies[3], head_lanes[3])
     up_b.finish2()
-    for copy in res_far + pair0 + pair1:
+    local_out.wait()
+    for copies in arriving:
+        for copy in copies:
+            copy.wait_recv()
+
+    def project_first(n, carry):
+        lanes = pl.ds(pl.multiple_of(n * 256, 256), 256)
+        upv[n] = res[:, :, lanes].reshape(512, 256).astype(F32) + jnp.dot(
+            attn[:, :, 0:768].reshape(512, 768), owb[0:768, lanes], preferred_element_type=F32
+        )
+        return carry
+
+    lax.fori_loop(0, 8, project_first, 0)
+    for copy in last:
         copy.wait_recv()
-    local_out.wait()
 
     def project(n, square):
         lanes = pl.ds(pl.multiple_of(n * 256, 256), 256)
-        part = res[:, :, lanes].reshape(512, 256).astype(F32) + jnp.dot(
-            attn[...].reshape(512, 1024), owb[:, lanes], preferred_element_type=F32
+        part = upv[n] + jnp.dot(
+            attn[:, :, 768:1024].reshape(512, 256), owb[768:1024, lanes], preferred_element_type=F32
         )
-        hid[:, lanes] = part
+        upv[n] = part
+        hid[:, lanes] = part[0:128]
         return square + jnp.sum(part * part, axis=1, keepdims=True)
 
     square = lax.fori_loop(0, 8, project, jnp.zeros((512, 1), F32))
+    gate_a.relay2()
+    down_a.turn()
     scale = lax.rsqrt(square * (1.0 / 2048) + EPSILON)
 
     def normalize(n, carry):
         lanes = pl.ds(pl.multiple_of(n * 256, 256), 256)
-        xn[:, lanes] = (hid[:, lanes] * scale * gain_in[:, lanes]).astype(BF16)
+        xn[:, lanes] = (upv[n] * scale * gain_in[:, lanes]).astype(BF16)
         return carry
 
     lax.fori_loop(0, 8, normalize, 0)
-
+    down_b.finish1()
+    gate_b.relay2()
+    down_b.turn()
     up_a.ready()
     up_b.ready()
 
+    def unit_columns(i):
+        return i // 2, pl.ds(pl.multiple_of(lax.rem(i, 2) * 256, 256), 256)
+
     def up_units(i, carry):
-        block, cols = i // 2, pl.ds(pl.multiple_of(lax.rem(i, 2) * 256, 256), 256)
+        block, cols = unit_columns(i)
         upv[i] = jnp.dot(
             xn[...], wu[block, :, :, :, cols].reshape(2048, 256), preferred_element_type=F32
         )
         return carry
 
-    lax.fori_loop(0, 4, up_units, 0)
-    gate_a.relay2()
-    down_a.turn()
-    down_b.finish1()
-    lax.fori_loop(4, 8, up_units, 0)
-    gate_b.relay2()
-    down_b.turn()
+    lax.fori_loop(0, 8, up_units, 0)
     gate_a.finish2()
     gate_b.finish2()
     gate_a.ready()
     gate_b.ready()
 
     def gate_units(i, carry):
-        block, cols = i // 2, pl.ds(pl.multiple_of(lax.rem(i, 2) * 256, 256), 256)
+        block, cols = unit_columns(i)
         g = jnp.dot(
             xn[...], wg[block, :, :, :, cols].reshape(2048, 256), preferred_element_type=F32
         )
         act[:, pl.ds(pl.multiple_of(i * 256, 256), 256)] = (
             g / (1.0 + jnp.exp(-g)) * upv[i]
         ).astype(BF16)
+
+        @pl.when(i == 5)
+        def _():
+            down_a.relay2()
+
         return carry
 
     lax.fori_loop(0, 8, gate_units, 0)
+    down_b.ready(1)
 
     half0, half1 = pl.ds(0, 64), pl.ds(64, 64)
-    hops, returns = {}, []
-
-    def block_sums(half, i):
-        weight = (wda, wdb)[half]
-        part = jnp.dot(
-            act[...],
-            jnp.concatenate([weight[0, i].reshape(2048, 128), weight[1, i].reshape(2048, 128)], axis=1),
-            preferred_element_type=F32,
-        )
-        n = half * 4 + i
-        acc[n] = part[0:128]
-        ends[0, n] = part[128:256]
-        ends[1, n] = part[384:512]
-        far[n] = part[256:384].astype(BF16)
-        hops[len(hops)] = (
-            n,
-            send(far.at[n, half0], hop.at[0, n], zs[1]),
-            send(far.at[n, half1], hop.at[1, n], zs[-1]),
-        )
-
-    def pass_on(k):
-        n, a, b = hops[k]
-        a.wait_recv()
-        near[0, n, 0:64] = (ends[0, n, 0:64] + hop[0, n].astype(F32)).astype(BF16)
-        near[0, n, 64:128] = ends[0, n, 64:128].astype(BF16)
-        returns.append(send(near.at[0, n], back.at[0, n], zs[1]))
-        b.wait_recv()
-        near[1, n, 0:64] = ends[1, n, 0:64].astype(BF16)
-        near[1, n, 64:128] = (ends[1, n, 64:128] + hop[1, n].astype(F32)).astype(BF16)
-        returns.append(send(near.at[1, n], back.at[1, n], zs[-1]))
-
-    before, after, opposite = [lax.rem(x + k, 4) for k in (3, 1, 2)]
-    down_b.ready(1)
-    block_sums(1, x)
-    down_b.relay2()
-    down_a.relay2()
-    down_b.ready(2)
-    block_sums(1, before)
-    pass_on(0)
-    block_sums(1, after)
-    pass_on(1)
-    down_a.finish2()
-    down_a.ready()
-    for step, i in enumerate((x, before, after, opposite)):
-        block_sums(0, i)
-        pass_on(2 + step)
-    down_b.finish2()
-    down_b.ready()
-    block_sums(1, opposite)
-    pass_on(6)
-    pass_on(7)
-
-    for copy in returns:
-        copy.wait_recv()
+    first_hop = counter[0]
+    counter[0] += 32
+
+    def place(k):
+        kind = 1 - lax.rem((k + 1) // 4, 2)
+        i = lax.rem(x + k + k // 2, 4) * kind + (k - 3) * (1 - kind)
+        return kind, i, kind * 4 + i
+
+    def hop_copies(k):
+        n = place(k)[2]
+        return [
+            pltpu.make_async_remote_copy(
+                src_ref=src, dst_ref=dst, send_sem=ssem.at[first_hop + j * 8 + k],
+                recv_sem=rsem.at[first_hop + j * 8 + k], device_id=device, device_id_type=MESH,
+            )
+            for j, (src, dst, device) in enumerate((
+                (far.at[n, half0], hop.at[0, n], zs[1]),
+                (far.at[n, half1], hop.at[1, n], zs[-1]),
+                (near.at[0, n], back.at[0, n], zs[1]),
+                (near.at[1, n], back.at[1, n], zs[-1]),
+            ))
+        ]
+
+    def down_step(k, carry):
+        @pl.when(k == 1)
+        def _():
+            down_b.relay2()
+            down_b.ready(2)
+
+        @pl.when(k == 3)
+        def _():
+            down_a.finish2()
+            down_a.ready()
+
+        @pl.when(k == 7)
+        def _():
+            down_b.finish2()
+            down_b.ready()
+
+        @pl.when(k < 8)
+        def _():
+            kind, i, n = place(k)
+            weight = jnp.concatenate(
+                [wd[kind, 0, i].reshape(2048, 128), wd[kind, 1, i].reshape(2048, 128)], axis=1
+            )
+            part = jnp.dot(act[...], weight, preferred_element_type=F32)
+            far[n] = part[256:384].astype(BF16)
+            copies = hop_copies(k)
+            copies[0].start()
+            copies[1].start()
+            acc[n] = part[0:128]
+            ends[0, n] = part[128:256]
+            ends[1, n] = part[384:512]
+
+        @pl.when(k > 0)
+        def _():
+            n = place(k - 1)[2]
+            copies = hop_copies(k - 1)
+            copies[0].wait_recv()
+            near[0, n, 0:64] = (ends[0, n, 0:64] + hop[0, n].astype(F32)).astype(BF16)
+            near[0, n, 64:128] = ends[0, n, 64:128].astype(BF16)
+            copies[2].start()
+            copies[1].wait_recv()
+            near[1, n, 0:64] = ends[1, n, 0:64].astype(BF16)
+            near[1, n, 64:128] = (ends[1, n, 64:128] + hop[1, n].astype(F32)).astype(BF16)
+            copies[3].start()
+
+        return carry
+
+    lax.fori_loop(0, 9, down_step, 0)
+
+    for k in range(8):
+        copies = hop_copies(k)
+        copies[2].wait_recv()
+        copies[3].wait_recv()
+        started.extend(copies)
     for half in range(2):
         for i in range(4):
             n = half * 4 + i
             total = acc[n] + back[0, n].astype(F32) + back[1, n].astype(F32)
             for cc in range(2):
                 lanes = slice(512 * i + 256 * cc + 128 * half, 512 * i + 256 * cc + 128 * half + 128)
-                out[:, lanes] = (hid[0:128, lanes] + total[:, 128 * cc:128 * cc + 128]).astype(BF16)
+                out[:, lanes] = (hid[:, lanes] + total[:, 128 * cc:128 * cc + 128]).astype(BF16)
 
     for copy in started:
         copy.wait_send()
@@ -487,12 +571,11 @@
             pltpu.VMEM((4, 128, 1024), BF16),
             pltpu.VMEM((1024, 2048), BF16),
             pltpu.VMEM((4, 128, 2048), BF16),
-            pltpu.VMEM((512, 2048), F32),
+            pltpu.VMEM((128, 2048), F32),
             pltpu.VMEM((512, 2048), BF16),
             pltpu.VMEM((4, 4, 2, 256, 512), BF16),
             pltpu.VMEM((4, 4, 2, 256, 512), BF16),
-            pltpu.VMEM((2, 4, 4, 512, 128), BF16),
-            pltpu.VMEM((2, 4, 4, 512, 128), BF16),
+            pltpu.VMEM((2, 2, 4, 4, 512, 128), BF16),
             pltpu.VMEM((8, 512, 256), F32),
             pltpu.VMEM((512, 2048), BF16),
             pltpu.VMEM((8, 128, 256), F32),

time: 142 us -> 116 us (0.82)
  Pallas kernels: 140 us -> 114 us
    pallas_call x1, Pallas kernels: 140 us -> 114 us  [shards(): pl.pallas_call(kernel, out_shape=jax.ShapeDtypeStruct((128, 2048), BF16),...]
where the time goes in v3:
time: 116 us
  Pallas kernels  114 us (98%)
  local copies, waits for them, and re-layouts  1.88 us (2%)
    pallas_call x1, Pallas kernels, shards(): pl.pallas_call(kernel, out_shape=jax.ShapeDtypeStruct((128, 2048), BF16),...  114 us

profile of v3, /device:TPU:0, one launch (start us, length us, event | category | flops | bytes accessed | tf_op | source)
XLA Modules:
  0.0 116.0 jit_solution(8172707897322396158)
XLA Ops:
  0.0 114.1 %shard_map.136 = bf16[128,2048]{1,0:T(8,128)(2,1)} custom-call(bf16[128,2048]{1,0:T(8,128)(2,1)} %res_in.1, bf16[128,1024]{1,0:T(8,128)(2,1)} %q_in.1, bf16[128,256]{1,0:T(8,128)(2,1)} %k_in.1, bf16[128,256]{1,0:T(8,128)(2,1)} %v_in.1, bf16[4,64,256]{2,1,0:T(8,128)(2,1)} %pk_in.1, bf16[4,64,256]{2,1,0:T(8,128)(2,1)} %pv_in.1, bf16[1024,2048]{1,0:T(8,128)(2,1)} %ow_in.1, ...), custom_call_target="tpu_custom_call" | custom-call | tf_op jit(solution)/shard_map/pallas_call | solution.py:552
  114.1 1.9 %copy.16 = bf16[128,2048]{1,0:T(8,128)(2,1)} copy(bf16[128,2048]{1,0:T(8,128)(2,1)} %shard_map.136) | data formatting | bytes 1048576

commit v4 on v3

--- a/solution.py
+++ b/solution.py
@@ -360,10 +360,10 @@
     arriving = [onward(res, res_copies[0], res_lanes[0])]
     arriving.append(onward(res, res_copies[1], res_lanes[1]))
     gate_b.relay1()
-    gate_a.turn()
     head(2)
     attn_copies.append(spread_z(attn, head_lanes[2]))
     down_b.relay1()
+    gate_a.turn()
     arriving.append(onward(attn, attn_copies[0], head_lanes[0]))
     gate_b.finish1()
     gate_b.turn()
@@ -382,11 +382,24 @@
         for copy in copies:
             copy.wait_recv()
 
+    down_b.finish1()
+
     def project_first(n, carry):
         lanes = pl.ds(pl.multiple_of(n * 256, 256), 256)
         upv[n] = res[:, :, lanes].reshape(512, 256).astype(F32) + jnp.dot(
             attn[:, :, 0:768].reshape(512, 768), owb[0:768, lanes], preferred_element_type=F32
         )
+
+        @pl.when(n == 4)
+        def _():
+            gate_a.relay2()
+            down_a.turn()
+
+        @pl.when(n == 7)
+        def _():
+            gate_b.relay2()
+            down_b.turn()
+
         return carry
 
     lax.fori_loop(0, 8, project_first, 0)
@@ -403,8 +416,6 @@
         return square + jnp.sum(part * part, axis=1, keepdims=True)
 
     square = lax.fori_loop(0, 8, project, jnp.zeros((512, 1), F32))
-    gate_a.relay2()
-    down_a.turn()
     scale = lax.rsqrt(square * (1.0 / 2048) + EPSILON)
 
     def normalize(n, carry):
@@ -413,9 +424,6 @@
         return carry
 
     lax.fori_loop(0, 8, normalize, 0)
-    down_b.finish1()
-    gate_b.relay2()
-    down_b.turn()
     up_a.ready()
     up_b.ready()
 
@@ -427,11 +435,18 @@
         upv[i] = jnp.dot(
             xn[...], wu[block, :, :, :, cols].reshape(2048, 256), preferred_element_type=F32
         )
+
+        @pl.when(i == 3)
+        def _():
+            gate_a.finish2()
+
+        @pl.when(i == 5)
+        def _():
+            gate_b.finish2()
+
         return carry
 
     lax.fori_loop(0, 8, up_units, 0)
-    gate_a.finish2()
-    gate_b.finish2()
     gate_a.ready()
     gate_b.ready()
 
@@ -444,7 +459,7 @@
             g / (1.0 + jnp.exp(-g)) * upv[i]
         ).astype(BF16)
 
-        @pl.when(i == 5)
+        @pl.when(i == 4)
         def _():
             down_a.relay2()
 
@@ -477,20 +492,39 @@
             ))
         ]
 
+    def pass_on(k):
+        n = place(k)[2]
+        copies = hop_copies(k)
+        copies[0].wait_recv()
+        near[0, n, 0:64] = (ends[0, n, 0:64] + hop[0, n].astype(F32)).astype(BF16)
+        near[0, n, 64:128] = ends[0, n, 64:128].astype(BF16)
+        copies[2].start()
+        copies[1].wait_recv()
+        near[1, n, 0:64] = ends[1, n, 0:64].astype(BF16)
+        near[1, n, 64:128] = (ends[1, n, 64:128] + hop[1, n].astype(F32)).astype(BF16)
+        copies[3].start()
+
     def down_step(k, carry):
         @pl.when(k == 1)
         def _():
             down_b.relay2()
+            pass_on(0)
             down_b.ready(2)
 
+        @pl.when(k == 2)
+        def _():
+            down_a.finish2()
+
         @pl.when(k == 3)
         def _():
-            down_a.finish2()
             down_a.ready()
 
+        @pl.when(k == 4)
+        def _():
+            down_b.finish2()
+
         @pl.when(k == 7)
         def _():
-            down_b.finish2()
             down_b.ready()
 
         @pl.when(k < 8)
@@ -508,35 +542,28 @@
             ends[0, n] = part[128:256]
             ends[1, n] = part[384:512]
 
-        @pl.when(k > 0)
-        def _():
-            n = place(k - 1)[2]
-            copies = hop_copies(k - 1)
-            copies[0].wait_recv()
-            near[0, n, 0:64] = (ends[0, n, 0:64] + hop[0, n].astype(F32)).astype(BF16)
-            near[0, n, 64:128] = ends[0, n, 64:128].astype(BF16)
-            copies[2].start()
-            copies[1].wait_recv()
-            near[1, n, 0:64] = ends[1, n, 0:64].astype(BF16)
-            near[1, n, 64:128] = (ends[1, n, 64:128] + hop[1, n].astype(F32)).astype(BF16)
-            copies[3].start()
+        @pl.when(k > 2)
+        def _():
+            pass_on(k - 2)
 
         return carry
 
-    lax.fori_loop(0, 9, down_step, 0)
-
-    for k in range(8):
+    lax.fori_loop(0, 10, down_step, 0)
+
+    def collect(k, carry):
         copies = hop_copies(k)
         copies[2].wait_recv()
         copies[3].wait_recv()
-        started.extend(copies)
-    for half in range(2):
-        for i in range(4):
-            n = half * 4 + i
-            total = acc[n] + back[0, n].astype(F32) + back[1, n].astype(F32)
-            for cc in range(2):
-                lanes = slice(512 * i + 256 * cc + 128 * half, 512 * i + 256 * cc + 128 * half + 128)
-                out[:, lanes] = (hid[:, lanes] + total[:, 128 * cc:128 * cc + 128]).astype(BF16)
+        kind, i, n = place(k)
+        total = acc[n] + back[0, n].astype(F32) + back[1, n].astype(F32)
+        for cc in range(2):
+            lanes = pl.ds(pl.multiple_of(512 * i + 256 * cc + 128 * kind, 128), 128)
+            out[:, lanes] = (hid[:, lanes] + total[:, 128 * cc:128 * cc + 128]).astype(BF16)
+        return carry
+
+    lax.fori_loop(0, 8, collect, 0)
+    for k in range(8):
+        started.extend(hop_copies(k))
 
     for copy in started:
         copy.wait_send()

time: 116 us -> 114 us (0.983)
  Pallas kernels: 114 us -> 111 us
    pallas_call x1, Pallas kernels: 114 us -> 111 us  [shards(): pl.pallas_call(kernel, out_shape=jax.ShapeDtypeStruct((128, 2048), BF16),...]
where the time goes in v4:
time: 114 us; the launch traced here: 113 us
  Pallas kernels  111 us (97%)
  local copies, waits for them, and re-layouts  1.88 us (2%)
    pallas_call x1, Pallas kernels, shards(): pl.pallas_call(kernel, out_shape=jax.ShapeDtypeStruct((128, 2048), BF16),...  111 us

profile of v4, /device:TPU:0, one launch (start us, length us, event | category | flops | bytes accessed | tf_op | source)
XLA Modules:
  0.0 113.1 jit_solution(10901978838269211797)
XLA Ops:
  0.0 111.2 %shard_map.136 = bf16[128,2048]{1,0:T(8,128)(2,1)} custom-call(bf16[128,2048]{1,0:T(8,128)(2,1)} %res_in.1, bf16[128,1024]{1,0:T(8,128)(2,1)} %q_in.1, bf16[128,256]{1,0:T(8,128)(2,1)} %k_in.1, bf16[128,256]{1,0:T(8,128)(2,1)} %v_in.1, bf16[4,64,256]{2,1,0:T(8,128)(2,1)} %pk_in.1, bf16[4,64,256]{2,1,0:T(8,128)(2,1)} %pv_in.1, bf16[1024,2048]{1,0:T(8,128)(2,1)} %ow_in.1, ...), custom_call_target="tpu_custom_call" | custom-call | tf_op jit(solution)/shard_map/pallas_call | solution.py:579
  111.3 1.9 %copy.16 = bf16[128,2048]{1,0:T(8,128)(2,1)} copy(bf16[128,2048]{1,0:T(8,128)(2,1)} %shard_map.136) | data formatting | bytes 1048576

commit v5 on v4

--- a/solution.py
+++ b/solution.py
@@ -173,15 +173,16 @@
     def quarter(lo, h):
         return pl.ds(lo + 64 * h, 64)
 
+    more, less = pl.ds(0, 144), pl.ds(144, 112)
     gate_a = Piece(
-        Ring(xs, x, lambda i: wg.at[y, i, c, top], lambda i, h: wg.at[y, i, c, quarter(0, h)]),
-        Ring(ys, y, lambda i: wg.at[i, :, c, top], lambda i, h: wg.at[i, pl.ds(2 * h, 2), c, top]),
-        wg_in.at[top], local_gate,
+        Ring(xs, x, lambda i: wg.at[y, i, c, more], lambda i, h: wg.at[y, i, c, (pl.ds(0, 80), pl.ds(80, 64))[h]]),
+        Ring(ys, y, lambda i: wg.at[i, :, c, more], lambda i, h: wg.at[i, pl.ds(2 * h, 2), c, more]),
+        wg_in.at[more], local_gate,
     )
     gate_b = Piece(
-        Ring(ys, y, lambda i: wg.at[i, x, c, bottom], lambda i, h: wg.at[i, x, c, quarter(128, h)]),
-        Ring(xs, x, lambda i: wg.at[:, i, c, bottom], lambda i, h: wg.at[pl.ds(2 * h, 2), i, c, bottom]),
-        wg_in.at[bottom], None,
+        Ring(ys, y, lambda i: wg.at[i, x, c, less], lambda i, h: wg.at[i, x, c, (pl.ds(144, 64), pl.ds(208, 48))[h]]),
+        Ring(xs, x, lambda i: wg.at[:, i, c, less], lambda i, h: wg.at[pl.ds(2 * h, 2), i, c, less]),
+        wg_in.at[less], None,
     )
     up_a = Piece(
         Ring(ys, y, lambda i: wu.at[i, x, c, top], lambda i, h: wu.at[i, x, c, quarter(0, h)]),

time: 114 us -> 113 us (level)
  no operation moved by 1% of the time
where the time goes in v5:
time: 113 us; the launch traced here: 112 us
  Pallas kernels  110 us (97%)
  local copies, waits for them, and re-layouts  1.88 us (2%)
    pallas_call x1, Pallas kernels, shards(): pl.pallas_call(kernel, out_shape=jax.ShapeDtypeStruct((128, 2048), BF16),...  110 us

profile of v5, /device:TPU:0, one launch (start us, length us, event | category | flops | bytes accessed | tf_op | source)
XLA Modules:
  0.0 112.0 jit_solution(7175663505385775731)
XLA Ops:
  0.0 110.1 %shard_map.136 = bf16[128,2048]{1,0:T(8,128)(2,1)} custom-call(bf16[128,2048]{1,0:T(8,128)(2,1)} %res_in.1, bf16[128,1024]{1,0:T(8,128)(2,1)} %q_in.1, bf16[128,256]{1,0:T(8,128)(2,1)} %k_in.1, bf16[128,256]{1,0:T(8,128)(2,1)} %v_in.1, bf16[4,64,256]{2,1,0:T(8,128)(2,1)} %pk_in.1, bf16[4,64,256]{2,1,0:T(8,128)(2,1)} %pv_in.1, bf16[1024,2048]{1,0:T(8,128)(2,1)} %ow_in.1, ...), custom_call_target="tpu_custom_call" | custom-call | tf_op jit(solution)/shard_map/pallas_call | solution.py:580
  110.1 1.9 %copy.16 = bf16[128,2048]{1,0:T(8,128)(2,1)} copy(bf16[128,2048]{1,0:T(8,128)(2,1)} %shard_map.136) | data formatting | bytes 1048576
